TPU v7x, 32 devices: a whole 2x2x4 slice. The times are simulated.
32 devices in a mesh: dp: 8 (over y, x, core), exch: 4 (over z).
Axes of the slice: x: 2, y: 2, z: 4, core: 2. Of those that a mesh axis runs over, the one named last changes fastest.
Arguments:
- x_raw: bfloat16 [1024, 2048], P('exch', 'dp'), may hold values from -6 to 6
- bc_raw: bfloat16 [1024, 256], P(('exch', 'dp')), may hold values from -6 to 6
- dt_raw: bfloat16 [32, 1024], P('dp', 'exch'), may hold values from -4 to 4
- cotangent: bfloat16 [1024, 2048], P('exch', 'dp'), may hold values from -6 to 6
- ssm_state: bfloat16 [8, 32, 64, 128], P('exch', 'dp'), may hold values from -0.625 to 0.625
- conv_x_state: bfloat16 [8, 3, 2048], P('exch', None, 'dp'), may hold values from -6 to 6
- conv_bc_state: bfloat16 [8, 3, 256], P('exch'), may hold values from -6 to 6
- owner: int32 [8], P('exch'), may hold values from 0 to 3, as said below
- resp_len: int32 [8], P('exch'), may hold values from 32 to 128, as said below
- conv_x_weight: float32 [4, 2048], P(None, 'dp'), may hold values from -3 to 3
- conv_bc_weight: float32 [4, 256], replicated, may hold values from -3 to 3
- dt_bias: float32 [32], P('dp'), may hold values from -5 to -3
- a_log: float32 [32], P('dp'), may hold values from -2.3 to 2.1
- skip_d: float32 [32], P('dp'), may hold values from 0.5 to 1.5
Outputs:
- grad_x: bfloat16 [1024, 2048], P('exch', 'dp')
- grad_bc: bfloat16 [1024, 256], P(('exch', 'dp'))
- grad_dt: bfloat16 [32, 1024], P('dp', 'exch')
- grad_conv_x: float32 [4, 2048], P(None, 'dp')
- grad_conv_bc: float32 [4, 256], replicated
- grad_heads: float32 [3, 32], P(None, 'dp')
Inputs may be any that keep to these rules, and one draw needn't show every extreme that they name: `owner`: among the 2 prompts of one holder (an aligned block along exch) no learner index occurs more than 1 times, and some learner index occurs exactly 1 times; over all 8 prompts every learner index occurs exactly 2 times. `resp_len`: every learner's block of 2 responses holds a response of length 128.
All inputs are finite; a program needn't handle non-finite values.
Results may differ from a plain program's by a relative error of at most 0.001.
Values may be sent and summed in bfloat16 or wider, within the bound.
A program may use at most 64 MiB of HBM per device.

v0:
```python
import functools

import jax
import jax.numpy as jnp
from jax import lax
from jax.experimental import pallas as pl
from jax.experimental.pallas import tpu as pltpu
from jax.sharding import PartitionSpec as P

DEV_GROUP = 8
GROUP = 1
MESH = pl.DeviceIdType.MESH
F32 = jnp.float32
BF16 = jnp.bfloat16


def nn(a, b):
    return lax.dot_general(a, b, (((1,), (0,)), ((), ())), preferred_element_type=F32)


def nt(a, b):
    return lax.dot_general(a, b, (((1,), (1,)), ((), ())), preferred_element_type=F32)


def split(a):
    high = a.astype(BF16)
    return high, (a - high.astype(F32)).astype(BF16)


def three(dot, a, b):
    return dot(a[0], b[0]) + (dot(a[0], b[1]) + dot(a[1], b[0]))


def iota(shape, dim):
    return lax.broadcasted_iota(jnp.int32, shape, dim)


def kernel(
    peers, slices, groups, *refs
):
    sources, refs = refs[:14], refs[14:]
    gx_ref, gbc_ref, gdt_ref, fin = refs[:4]
    inputs, refs = refs[4:18], refs[18:]
    owner, lens, bias, a_log, skip, x_ref, bc_ref, dt_ref, cot_ref = inputs[:9]
    ssm_ref, cx_ref, cbc_ref, wx_ref, wbc_ref = inputs[9:]
    (
    msg, state, gath, msg_out, state_out, pad_x, pad_bc, dpx, dpbc, dw_ref, taps, raw, back,
    sem_in, sem_msg, sem_state, sem_gath, sem_taps, sem_back, sem_wx, sem_heads, sem_fin,
    ) = refs
    mine = lax.axis_index("exch")
    me = lax.axis_index("dp")
    depth, prompts, channels = cx_ref.shape
    taps_n = depth + 1
    responses = lens.shape[0]
    heads = bias.shape[0]
    width = channels // heads
    tokens = x_ref.shape[0]
    length = tokens // responses
    rows = bc_ref.shape[0]
    pair = cbc_ref.shape[2]
    half = pair // 2
    lanes = responses * heads
    base = 8 - depth

    def along(offset):
        return {"exch": lax.rem(mine + offset, peers)}

    def across(offset):
        return {"dp": lax.rem(me + offset, slices)}

    barrier = pltpu.get_barrier_semaphore()
    for offset in range(1, slices):
        pl.semaphore_signal(barrier, inc=1, device_id=across(offset), device_id_type=MESH)
    for offset in range(1, peers):
        pl.semaphore_signal(barrier, inc=1, device_id=along(offset), device_id_type=MESH)

    loads = [
        pltpu.make_async_copy(src, dst, sem_in.at[i])
        for i, (src, dst) in enumerate(zip(sources, inputs))
    ]
    sooner = (0, 10, 11, 9, 6)
    later = [i for i in range(len(loads)) if i not in sooner]
    for i in sooner:
        loads[i].start()
    for i in later:
        loads[i].start()
    for i in sooner:
        loads[i].wait()

    tails = [
        jnp.concatenate([cx_ref[k].astype(F32), cbc_ref[k].astype(F32)], axis=1)
        for k in range(depth)
    ]

    def fill(target, msg_dst, state_dst):
        small = [jnp.zeros((1, channels + pair), F32)] * depth
        flag = jnp.zeros((1, channels + pair), F32)
        big = jnp.zeros(ssm_ref.shape[1:], F32)
        for p in range(prompts):
            weight = (owner[p] == target).astype(F32)
            for k in range(depth):
                small[k] = small[k] + tails[k][p : p + 1] * weight
            flag = flag + weight
            big = big + ssm_ref[p].astype(F32) * weight
        msg_dst[...] = jnp.concatenate(small + [flag], axis=0).astype(BF16)
        state_dst[...] = big.astype(BF16)

    for offset in range(1, peers):
        fill(lax.rem(mine + offset, peers), msg_out.at[offset], state_out.at[offset])
    fill(mine, msg.at[mine], state.at[mine])

    pl.semaphore_wait(barrier, slices - 1 + peers - 1)

    def remote(src, dst, sem, offset, where):
        copy = pltpu.make_async_remote_copy(
            src_ref=src,
            dst_ref=dst,
            send_sem=sem.at[0, offset],
            recv_sem=sem.at[1, offset],
            device_id=where,
            device_id_type=MESH,
        )
        copy.start()
        return copy

    def group_columns(ref, who):
        if groups == 1:
            return ref
        start = pl.multiple_of((who // DEV_GROUP) * pair, pair)
        return ref.at[:, pl.ds(start, pair)]

    msg_copies = [
        remote(msg_out.at[o], msg.at[mine], sem_msg, o, along(o)) for o in range(1, peers)
    ]
    gath_copies = [
        remote(
            group_columns(bc_ref, lax.rem(me + o, slices)),
            gath.at[me],
            sem_gath,
            o,
            across(o),
        )
        for o in range(1, slices)
    ]
    state_copies = [
        remote(state_out.at[o], state.at[mine], sem_state, o, along(o))
        for o in range(peers - 1, 0, -1)
    ]
    gath[me] = group_columns(bc_ref, me)[...]

    for i in later:
        loads[i].wait()

    row_head = lax.rem(iota((lanes, 1), 0), heads)

    def per_row(ref):
        out = jnp.zeros((lanes, 1), F32)
        for h in range(heads):
            out = jnp.where(row_head == h, ref[h], out)
        return out

    lane_head = iota((1, channels), 1) // width
    skip_row = jnp.zeros((1, channels), F32)
    for h in range(heads):
        skip_row = jnp.where(lane_head == h, skip[h], skip_row)
    dt_in = jnp.concatenate(
        [dt_ref[:, r * length : (r + 1) * length].astype(F32) for r in range(responses)], axis=0
    )
    dt_pre = dt_in + per_row(bias)
    small = jnp.exp(-jnp.abs(dt_pre))
    above = 1.0 + small
    log1p = jnp.where(above == 1.0, small, jnp.log(above) * (small / (above - 1.0)))
    dt = jnp.maximum(dt_pre, 0.0) + log1p
    rate = jnp.exp(per_row(a_log))
    first = iota((length, length), 0)
    second = iota((length, length), 1)
    upto = (first <= second).astype(F32)
    onward = (first >= second).astype(F32)
    causal = first <= second
    logs = lax.dot_general(
        -rate * dt,
        upto,
        (((1,), (0,)), ((), ())),
        preferred_element_type=F32,
        precision=lax.Precision.HIGHEST,
    )
    entry = jnp.exp(logs)
    logs_col = logs.T
    dt_col = dt.T
    entry_col = entry.T

    def spread_heads(cols, r):
        parts = [
            jnp.broadcast_to(cols[:, r * heads + h : r * heads + h + 1], (length, width))
            for h in range(heads)
        ]
        return jnp.concatenate(parts, axis=1)

    def indicator(r):
        row = iota((lanes, channels), 0)
        head = iota((lanes, channels), 1) // width
        return (row == r * heads + head).astype(BF16)

    for r in range(responses):
        block = slice(r * length, (r + 1) * length)
        pad_x[r, 8 : 8 + length] = x_ref[block].astype(F32)
    cots = []
    for r in range(responses):
        block = slice(r * length, (r + 1) * length)
        live = iota((length, 1), 0) < lens[r]
        cots.append(jnp.where(live, cot_ref[block].astype(F32), 0.0))

    for copy in msg_copies:
        copy.wait_recv()
    got = [msg[z].astype(F32) for z in range(peers)]
    weights = [[None] * peers for _ in range(prompts)]
    seen = jnp.zeros((1, channels + pair), F32)
    for z in range(peers):
        present = got[z][depth : depth + 1]
        for j in range(prompts):
            weights[j][z] = jnp.where(seen == float(j), present, 0.0)
        seen = seen + present
    for r in range(responses):
        prev = jnp.zeros((depth, channels + pair), F32)
        for z in range(peers):
            prev = prev + got[z][0:depth] * weights[r // GROUP][z]
        pad_x[r, base:8] = prev[:, :channels]
        pad_bc[r, base:8] = prev[:, channels:]

    def convolve(pad, weight, r):
        pre = pad[r, base : base + length] * weight[0:1]
        for k in range(1, taps_n):
            pre = pre + pad[r, base + k : base + k + length] * weight[k : k + 1]
        gate = 1.0 / (1.0 + jnp.exp(-pre))
        return pre * gate, gate * (1.0 + pre * (1.0 - gate))

    wx = wx_ref[...]
    wbc = wbc_ref[...]
    x_acts = [convolve(pad_x, wx, r) for r in range(responses)]

    for copy in gath_copies:
        copy.wait_recv()
    slots = length // rows
    for d in range(slices):
        r, place = d // slots, d % slots
        pad_bc[r, 8 + place * rows : 8 + (place + 1) * rows] = gath[d].astype(F32)
    bc_acts = [convolve(pad_bc, wbc, r) for r in range(responses)]

    across_rows = jnp.zeros((lanes, length), F32)
    dt_first = jnp.zeros((lanes, length), F32)
    row_index = iota((lanes, 1), 0)
    skip_sum = jnp.zeros((1, channels), F32)
    grad_wx = jnp.zeros((taps_n, channels), F32)
    b_grads, c_grads = [], []

    def weight_grad(grad, pad, r):
        parts = [
            jnp.sum(grad * pad[r, base + k : base + k + length], axis=0, keepdims=True)
            for k in range(taps_n)
        ]
        return jnp.concatenate(parts, axis=0)

    def input_grad(ref, weight, r):
        total = ref[r, depth : depth + length] * weight[0:1]
        for k in range(1, taps_n):
            total = total + ref[r, depth - k : depth - k + length] * weight[k : k + 1]
        return total

    for r in range(responses):
        act, slope = x_acts[r]
        cot = cots[r]
        cot_b = cot.astype(BF16)
        dt_full = spread_heads(dt_col, r)
        weighted = split(act * dt_full)
        proj_b = split(bc_acts[r][0][:, :half])
        proj_c = split(bc_acts[r][0][:, half:])
        scores = three(nt, proj_b, proj_c)
        score_grad = jnp.zeros((length, length), F32)
        for h in range(heads):
            i = r * heads + h
            cols = slice(h * width, (h + 1) * width)
            cot_h = cot_b[:, cols]
            gap = logs[i : i + 1] - logs_col[:, i : i + 1]
            decay = jnp.where(causal, jnp.exp(jnp.where(causal, gap, 0.0)), 0.0)
            mix = scores * decay
            mix_grad = nt(weighted[0][:, cols], cot_h) + nt(weighted[1][:, cols], cot_h)
            high, low = split(mix)
            dw_ref[r, :, cols] = nn(high, cot_h) + nn(low, cot_h)
            score_grad = score_grad + mix_grad * decay
            found = jnp.sum(mix_grad * mix, axis=0, keepdims=True)
            across_rows = jnp.where(row_index == i, found, across_rows)
        dw = dw_ref[r]
        prod = split(dw * act)
        mark = indicator(r)
        dt_first = dt_first + (nt(mark, prod[0]) + nt(mark, prod[1]))
        skip_sum = skip_sum + jnp.sum(cot * act, axis=0, keepdims=True)
        pre_grad = (dw * dt_full + skip_row * cot) * slope
        dpx[r, 0:length] = pre_grad
        dpx[r, length : length + 8] = jnp.zeros((8, channels), F32)
        grad_wx = grad_wx + weight_grad(pre_grad, pad_x, r)
        gx_ref[r * length : (r + 1) * length] = input_grad(dpx, wx, r).astype(BF16)
        b_grads.append(three(nn, split(score_grad), proj_c))
        c_grads.append(three(nn, split(score_grad.T), proj_b))

    def send_rows(row, sem):
        part = fin.at[mine, pl.ds(row, 8)]
        return [remote(part, part, sem, o, along(o)) for o in range(1, peers)]

    fin[mine] = jnp.zeros(fin.shape[1:], F32)
    fin[mine, 0:taps_n, 0:channels] = grad_wx
    fin_copies = send_rows(0, sem_wx)

    for copy in state_copies:
        copy.wait_recv()
    starts = []
    grad_taps = jnp.zeros((taps_n, pair), F32)
    for r in range(responses):
        start = jnp.zeros(state.shape[1:], F32)
        for z in range(peers):
            pick = weights[r // GROUP][z][:, : state.shape[2]]
            start = start + state[z].astype(F32) * pick
        start = start.astype(BF16)
        starts.append(start)
        fed = split(cots[r] * spread_heads(entry_col, r))
        c_grad = c_grads[r] + (nn(fed[0], start) + nn(fed[1], start))
        slope = bc_acts[r][1]
        pre_grad = jnp.concatenate([b_grads[r], c_grad], axis=1) * slope
        dpbc[r, 0:length] = pre_grad
        dpbc[r, length : length + 8] = jnp.zeros((8, pair), F32)
        grad_taps = grad_taps + weight_grad(pre_grad, pad_bc, r)

    taps[me, 0:taps_n] = grad_taps
    taps_copies = [
        remote(taps.at[me], taps.at[me], sem_taps, o, across(o)) for o in range(1, slices)
    ]
    for r in range(responses):
        block = input_grad(dpbc, wbc, r)
        for place in range(slots):
            raw[r * slots + place] = block[place * rows : (place + 1) * rows]
    back_copies = [
        remote(raw.at[lax.rem(me + o, slices)], back.at[me], sem_back, o, across(o))
        for o in range(1, slices)
    ]
    back[me] = raw[me]

    entry_grad = jnp.zeros((lanes, length), F32)
    for r in range(responses):
        proj_c = split(bc_acts[r][0][:, half:])
        carried = nt(proj_c[0], starts[r]) + nt(proj_c[1], starts[r])
        prod = split(carried * cots[r])
        mark = indicator(r)
        entry_grad = entry_grad + (nt(mark, prod[0]) + nt(mark, prod[1]))
    log_grad = across_rows + entry * entry_grad - dt * dt_first
    step_grad = lax.dot_general(
        log_grad,
        onward,
        (((1,), (0,)), ((), ())),
        preferred_element_type=F32,
        precision=lax.Precision.HIGHEST,
    )
    dt_grad = dt_first - rate * step_grad
    raw_grad = dt_grad * (1.0 / (1.0 + jnp.exp(-dt_pre)))
    for r in range(responses):
        gdt_ref[:, r * length : (r + 1) * length] = raw_grad[
            r * heads : (r + 1) * heads
        ].astype(BF16)
    bias_rows = jnp.sum(raw_grad, axis=1, keepdims=True)
    decay_rows = -rate * jnp.sum(dt * step_grad, axis=1, keepdims=True)
    bias_grad = jnp.zeros((heads, 1), F32)
    decay_grad = jnp.zeros((heads, 1), F32)
    for r in range(responses):
        bias_grad = bias_grad + bias_rows[r * heads : (r + 1) * heads]
        decay_grad = decay_grad + decay_rows[r * heads : (r + 1) * heads]
    own = iota((heads, channels), 0) == iota((heads, channels), 1) // width
    skip_grad = jnp.sum(jnp.where(own, skip_sum, 0.0), axis=1, keepdims=True)
    column = iota((heads, half), 1)
    head_block = jnp.where(
        column == 0,
        bias_grad,
        jnp.where(column == 1, decay_grad, jnp.where(column == 2, skip_grad, 0.0)),
    )
    fin[mine, 8 : 8 + heads, 0:half] = head_block
    fin_copies = fin_copies + send_rows(8, sem_heads)

    for copy in taps_copies:
        copy.wait_recv()
    for q in range(groups):
        total = taps[q * DEV_GROUP, 0:taps_n]
        for d in range(1, DEV_GROUP):
            total = total + taps[q * DEV_GROUP + d, 0:taps_n]
        fin[mine, 16 : 16 + taps_n, q * pair : (q + 1) * pair] = total
    fin_copies = fin_copies + send_rows(16, sem_fin)

    for copy in back_copies:
        copy.wait_recv()
    for q in range(groups):
        total = back[q * DEV_GROUP]
        for d in range(1, DEV_GROUP):
            total = total + back[q * DEV_GROUP + d]
        gbc_ref[:, q * pair : (q + 1) * pair] = total.astype(BF16)

    for copy in fin_copies:
        copy.wait_recv()
    for copy in msg_copies + gath_copies + state_copies + taps_copies + back_copies + fin_copies:
        copy.wait_send()


def finish(
    gx_in, gbc_in, gdt_in, fin, gx_ref, gbc_ref, gdt_ref, gwx_ref, gtaps_ref, gheads_ref, sems
):
    copies = [
        pltpu.make_async_copy(src, dst, sems.at[i])
        for i, (src, dst) in enumerate(
            ((gx_in, gx_ref), (gbc_in, gbc_ref), (gdt_in, gdt_ref))
        )
    ]
    for copy in copies:
        copy.start()
    taps_n, channels = gwx_ref.shape
    heads = gheads_ref.shape[1]
    pairs = gtaps_ref.shape[1]
    total = fin[0]
    for z in range(1, fin.shape[0]):
        total = total + fin[z]
    gwx_ref[...] = total[0:taps_n, 0:channels]
    gtaps_ref[...] = total[16 : 16 + taps_n, 0:pairs]
    gheads_ref[...] = total[8:16, 0:128].T[0:3, 0:heads]
    for copy in copies:
        copy.wait()


def local(
    x_raw, bc_raw, dt_raw, cotangent, ssm_state, conv_x_state, conv_bc_state, owner, resp_len,
    conv_x_weight, conv_bc_weight, dt_bias, a_log, skip_d,
):
    peers = lax.axis_size("exch")
    slices = lax.axis_size("dp")
    prompts, heads, width, nstate = ssm_state.shape
    channels = x_raw.shape[1]
    pair = 2 * nstate
    depth = conv_x_state.shape[1]
    responses = resp_len.shape[0]
    tokens = x_raw.shape[0]
    length = tokens // responses
    rows, all_pairs = bc_raw.shape
    groups = all_pairs // pair
    bc_state, bc_weight = conv_bc_state, conv_bc_weight
    if groups > 1:
        first = (lax.axis_index("dp") // DEV_GROUP) * pair
        bc_state = lax.dynamic_slice_in_dim(conv_bc_state, first, pair, 2)
        bc_weight = lax.dynamic_slice_in_dim(conv_bc_weight, first, pair, 1)
    ssm = ssm_state.reshape(prompts, heads * width, nstate)
    wide = max(all_pairs, channels)
    vmem = pl.BlockSpec(memory_space=pltpu.VMEM)
    dma = pltpu.SemaphoreType.DMA
    outs = (
        jax.ShapeDtypeStruct((tokens, channels), BF16),
        jax.ShapeDtypeStruct((rows, all_pairs), BF16),
        jax.ShapeDtypeStruct((heads, tokens), BF16),
        jax.ShapeDtypeStruct((depth + 1, channels), F32),
        jax.ShapeDtypeStruct((depth + 1, all_pairs), F32),
        jax.ShapeDtypeStruct((3, heads), F32),
    )
    staged = tuple(pltpu.VMEM(out.shape, out.dtype) for out in outs[:3])
    staged = staged + (pltpu.VMEM((peers, 24, wide), F32),)
    args = (
        owner, resp_len, dt_bias, a_log, skip_d, x_raw, bc_raw, dt_raw, cotangent, ssm,
        conv_x_state.transpose(1, 0, 2), bc_state.transpose(1, 0, 2), conv_x_weight, bc_weight,
    )
    held = pl.pallas_call(
        functools.partial(kernel, peers, slices, groups),
        out_shape=staged,
        in_specs=[pl.BlockSpec(memory_space=pltpu.HBM)] * 14,
        out_specs=[vmem] * 4,
        scratch_shapes=[pltpu.SMEM(a.shape, a.dtype) for a in args[:5]]
        + [pltpu.VMEM(a.shape, a.dtype) for a in args[5:]]
        + [
            pltpu.VMEM((peers, depth + 1, channels + pair), BF16),
            pltpu.VMEM((peers, heads * width, nstate), BF16),
            pltpu.VMEM((slices, rows, pair), BF16),
            pltpu.VMEM((peers, depth + 1, channels + pair), BF16),
            pltpu.VMEM((peers, heads * width, nstate), BF16),
            pltpu.VMEM((responses, length + 8, channels), F32),
            pltpu.VMEM((responses, length + 8, pair), F32),
            pltpu.VMEM((responses, length + 8, channels), F32),
            pltpu.VMEM((responses, length + 8, pair), F32),
            pltpu.VMEM((responses, length, channels), F32),
            pltpu.VMEM((slices, 8, pair), F32),
            pltpu.VMEM((slices, rows, pair), F32),
            pltpu.VMEM((slices, rows, pair), F32),
            dma((14,)),
            dma((2, peers)),
            dma((2, peers)),
            dma((2, slices)),
            dma((2, slices)),
            dma((2, slices)),
            dma((2, peers)),
            dma((2, peers)),
            dma((2, peers)),
        ],
        compiler_params=pltpu.CompilerParams(
            collective_id=0, has_side_effects=True
        ),
    )(*args)
    anywhere = pl.BlockSpec(memory_space=pl.ANY)
    return pl.pallas_call(
        finish,
        out_shape=outs,
        in_specs=[vmem] * 4,
        out_specs=[anywhere] * 3 + [vmem] * 3,
        scratch_shapes=[dma((3,))],
        compiler_params=pltpu.CompilerParams(vmem_limit_bytes=16 * 1024 * 1024),
    )(*held)


def solution(mesh):
    in_specs = (
        P("exch", "dp"),
        P(("exch", "dp"), None),
        P("dp", "exch"),
        P("exch", "dp"),
        P("exch", "dp", None, None),
        P("exch", None, "dp"),
        P("exch", None, None),
        P("exch"),
        P("exch"),
        P(None, "dp"),
        P(),
        P("dp"),
        P("dp"),
        P("dp"),
    )
    out_specs = (
        P("exch", "dp"),
        P(("exch", "dp"), None),
        P("dp", "exch"),
        P(None, "dp"),
        P(),
        P(None, "dp"),
    )
    return jax.shard_map(local, mesh=mesh, in_specs=in_specs, out_specs=out_specs, check_vma=False)
```

profile of v0, /device:TPU:0, one launch (start us, length us, event | category | flops | bytes accessed | tf_op | source)
XLA Modules:
  0.0 23.3 jit_solution(3392792940267017481)
XLA Ops:
  0.6 21.3 %shard_map.181 = (bf16[256,256]{1,0:T(8,128)(2,1)S(1)}, bf16[32,256]{1,0:T(8,128)(2,1)S(1)}, bf16[4,256]{1,0:T(4,128)(2,1)S(1)}, f32[4,24,256]{2,1,0:T(8,128)S(1)}) custom-call(s32[2]{0:T(128)} %refs_0_.1, s32[2]{0:T(128)} %refs_1_.1, f32[4]{0:T(128)} %refs_2_.1, f32[4]{0:T(128)} %refs_3_.1, f32[4]{0:T(128)} %refs_4_.1, bf16[256,256]{1,0:T(8,128)(2,1)} %refs_5_.1, ...), custom_call_target="tpu_custom_call" | custom-call | tf_op jit(solution)/shard_map/pallas_call | solution.py:470
  22.0 1.3 %shard_map.182 = (bf16[256,256]{1,0:T(8,128)(2,1)}, bf16[32,256]{1,0:T(8,128)(2,1)}, bf16[4,256]{1,0:T(4,128)(2,1)}, f32[4,256]{1,0:T(4,128)}, f32[4,256]{1,0:T(4,128)}, /*index=5*/f32[3,4]{1,0:T(4,128)}) custom-call(bf16[256,256]{1,0:T(8,128)(2,1)S(1)} %get-tuple-element.10.gx_in, bf16[32,256]{1,0:T(8,128)(2,1)S(1)} %get-tuple-element.11.gbc_in, ...), custom_call_target="tpu_custom_call" | custom-call | tf_op jit(solution)/shard_map/pallas_call | solution.py:506
where the time goes:
time: 23.4 us; the launch traced here: 23.3 us
  Pallas kernels  22.6 us (97%)
  between operations  0.65 us (3%)
    pallas_call x1, Pallas kernels, local(): pl.pallas_call(functools.partial(kernel, peers, slices, groups), out_shap...  21.3 us
    pallas_call x1, Pallas kernels, local(): pl.pallas_call(finish, out_shape=outs, in_specs=[vmem] * 4, out_specs=[an...  1.29 us

commit v1 on v0

--- a/solution.py
+++ b/solution.py
@@ -39,13 +39,14 @@
     peers, slices, groups, *refs
 ):
     sources, refs = refs[:14], refs[14:]
-    gx_ref, gbc_ref, gdt_ref, fin = refs[:4]
-    inputs, refs = refs[4:18], refs[18:]
+    gx_ref, gbc_ref, gdt_ref, gwx_ref, gtaps_ref, gheads_ref = refs[:6]
+    inputs, refs = refs[6:20], refs[20:]
     owner, lens, bias, a_log, skip, x_ref, bc_ref, dt_ref, cot_ref = inputs[:9]
     ssm_ref, cx_ref, cbc_ref, wx_ref, wbc_ref = inputs[9:]
     (
-    msg, state, gath, msg_out, state_out, pad_x, pad_bc, dpx, dpbc, dw_ref, taps, raw, back,
-    sem_in, sem_msg, sem_state, sem_gath, sem_taps, sem_back, sem_wx, sem_heads, sem_fin,
+    msg, state, gath, msg_out, state_out, pad_x, pad_bc, dpx, dpbc, dw_ref, raw, back,
+    fin, along_taps, across_taps,
+    sem_in, sem_msg, sem_state, sem_gath, sem_along, sem_across, sem_back, sem_fin,
     ) = refs
     mine = lax.axis_index("exch")
     me = lax.axis_index("dp")
@@ -69,59 +70,67 @@
         return {"dp": lax.rem(me + offset, slices)}
 
     barrier = pltpu.get_barrier_semaphore()
+    for offset in range(1, peers):
+        pl.semaphore_signal(barrier, inc=1, device_id=along(offset), device_id_type=MESH)
     for offset in range(1, slices):
         pl.semaphore_signal(barrier, inc=1, device_id=across(offset), device_id_type=MESH)
-    for offset in range(1, peers):
-        pl.semaphore_signal(barrier, inc=1, device_id=along(offset), device_id_type=MESH)
-
     loads = [
         pltpu.make_async_copy(src, dst, sem_in.at[i])
         for i, (src, dst) in enumerate(zip(sources, inputs))
     ]
-    sooner = (0, 10, 11, 9, 6)
+    sooner = (6, 0, 10, 11, 9)
     later = [i for i in range(len(loads)) if i not in sooner]
     for i in sooner:
         loads[i].start()
     for i in later:
         loads[i].start()
-    for i in sooner:
+    for i in sooner[:-1]:
         loads[i].wait()
-
     tails = [
         jnp.concatenate([cx_ref[k].astype(F32), cbc_ref[k].astype(F32)], axis=1)
         for k in range(depth)
     ]
 
-    def fill(target, msg_dst, state_dst):
+    def fill_msg(target, dst):
         small = [jnp.zeros((1, channels + pair), F32)] * depth
         flag = jnp.zeros((1, channels + pair), F32)
-        big = jnp.zeros(ssm_ref.shape[1:], F32)
         for p in range(prompts):
             weight = (owner[p] == target).astype(F32)
             for k in range(depth):
                 small[k] = small[k] + tails[k][p : p + 1] * weight
             flag = flag + weight
-            big = big + ssm_ref[p].astype(F32) * weight
-        msg_dst[...] = jnp.concatenate(small + [flag], axis=0).astype(BF16)
-        state_dst[...] = big.astype(BF16)
-
-    for offset in range(1, peers):
-        fill(lax.rem(mine + offset, peers), msg_out.at[offset], state_out.at[offset])
-    fill(mine, msg.at[mine], state.at[mine])
-
+        dst[...] = jnp.concatenate(small + [flag], axis=0).astype(BF16)
+
+    def fill_state(target, dst):
+        big = jnp.zeros(ssm_ref.shape[1:], F32)
+        for p in range(prompts):
+            big = big + ssm_ref[p].astype(F32) * (owner[p] == target).astype(F32)
+        dst[...] = big.astype(BF16)
+
+    low = 1 - (2 * mine) // peers
+    order = []
+    for k in range(peers - 1):
+        down = peers - 1 - k
+        down = down - (mine - down + peers) // peers
+        up = k + (k - mine + peers) // peers
+        order.append(low * down + (1 - low) * up)
+
+    for k in range(peers - 1):
+        fill_msg(order[k], msg_out.at[k])
+    fill_msg(mine, msg.at[mine])
     pl.semaphore_wait(barrier, slices - 1 + peers - 1)
-
-    def remote(src, dst, sem, offset, where):
-        copy = pltpu.make_async_remote_copy(
+    def remote(src, dst, sem, where):
+        pltpu.make_async_remote_copy(
             src_ref=src,
             dst_ref=dst,
-            send_sem=sem.at[0, offset],
-            recv_sem=sem.at[1, offset],
+            send_sem=sem.at[0],
+            recv_sem=sem.at[1],
             device_id=where,
             device_id_type=MESH,
-        )
-        copy.start()
-        return copy
+        ).start()
+
+    def settle(sem, which, ref):
+        pltpu.make_async_copy(ref, ref, sem.at[which]).wait()
 
     def group_columns(ref, who):
         if groups == 1:
@@ -129,28 +138,19 @@
         start = pl.multiple_of((who // DEV_GROUP) * pair, pair)
         return ref.at[:, pl.ds(start, pair)]
 
-    msg_copies = [
-        remote(msg_out.at[o], msg.at[mine], sem_msg, o, along(o)) for o in range(1, peers)
-    ]
-    gath_copies = [
-        remote(
-            group_columns(bc_ref, lax.rem(me + o, slices)),
-            gath.at[me],
-            sem_gath,
-            o,
-            across(o),
-        )
-        for o in range(1, slices)
-    ]
-    state_copies = [
-        remote(state_out.at[o], state.at[mine], sem_state, o, along(o))
-        for o in range(peers - 1, 0, -1)
-    ]
+    for k in range(peers - 1):
+        remote(msg_out.at[k], msg.at[mine], sem_msg, {"exch": order[k]})
+    for o in range(1, slices):
+        columns = group_columns(bc_ref, lax.rem(me + o, slices))
+        remote(columns, gath.at[me], sem_gath, across(o))
+    loads[sooner[-1]].wait()
+    for k in range(peers - 1):
+        fill_state(order[k], state_out.at[k])
+        remote(state_out.at[k], state.at[mine], sem_state, {"exch": order[k]})
+    fill_state(mine, state.at[mine])
     gath[me] = group_columns(bc_ref, me)[...]
-
     for i in later:
         loads[i].wait()
-
     row_head = lax.rem(iota((lanes, 1), 0), heads)
 
     def per_row(ref):
@@ -209,9 +209,7 @@
         block = slice(r * length, (r + 1) * length)
         live = iota((length, 1), 0) < lens[r]
         cots.append(jnp.where(live, cot_ref[block].astype(F32), 0.0))
-
-    for copy in msg_copies:
-        copy.wait_recv()
+    settle(sem_msg, 1, msg.at[pl.ds(0, peers - 1)])
     got = [msg[z].astype(F32) for z in range(peers)]
     weights = [[None] * peers for _ in range(prompts)]
     seen = jnp.zeros((1, channels + pair), F32)
@@ -237,15 +235,12 @@
     wx = wx_ref[...]
     wbc = wbc_ref[...]
     x_acts = [convolve(pad_x, wx, r) for r in range(responses)]
-
-    for copy in gath_copies:
-        copy.wait_recv()
+    settle(sem_gath, 1, gath.at[pl.ds(0, slices - 1)])
     slots = length // rows
     for d in range(slices):
         r, place = d // slots, d % slots
         pad_bc[r, 8 + place * rows : 8 + (place + 1) * rows] = gath[d].astype(F32)
     bc_acts = [convolve(pad_bc, wbc, r) for r in range(responses)]
-
     across_rows = jnp.zeros((lanes, length), F32)
     dt_first = jnp.zeros((lanes, length), F32)
     row_index = iota((lanes, 1), 0)
@@ -301,17 +296,7 @@
         gx_ref[r * length : (r + 1) * length] = input_grad(dpx, wx, r).astype(BF16)
         b_grads.append(three(nn, split(score_grad), proj_c))
         c_grads.append(three(nn, split(score_grad.T), proj_b))
-
-    def send_rows(row, sem):
-        part = fin.at[mine, pl.ds(row, 8)]
-        return [remote(part, part, sem, o, along(o)) for o in range(1, peers)]
-
-    fin[mine] = jnp.zeros(fin.shape[1:], F32)
-    fin[mine, 0:taps_n, 0:channels] = grad_wx
-    fin_copies = send_rows(0, sem_wx)
-
-    for copy in state_copies:
-        copy.wait_recv()
+    settle(sem_state, 1, state.at[pl.ds(0, peers - 1)])
     starts = []
     grad_taps = jnp.zeros((taps_n, pair), F32)
     for r in range(responses):
@@ -328,21 +313,16 @@
         dpbc[r, 0:length] = pre_grad
         dpbc[r, length : length + 8] = jnp.zeros((8, pair), F32)
         grad_taps = grad_taps + weight_grad(pre_grad, pad_bc, r)
-
-    taps[me, 0:taps_n] = grad_taps
-    taps_copies = [
-        remote(taps.at[me], taps.at[me], sem_taps, o, across(o)) for o in range(1, slices)
-    ]
+    along_taps[mine] = jnp.concatenate([grad_taps[:, :half], grad_taps[:, half:]], axis=0)
+    for o in range(1, peers):
+        remote(along_taps.at[mine], along_taps.at[mine], sem_along, along(o))
     for r in range(responses):
         block = input_grad(dpbc, wbc, r)
         for place in range(slots):
             raw[r * slots + place] = block[place * rows : (place + 1) * rows]
-    back_copies = [
-        remote(raw.at[lax.rem(me + o, slices)], back.at[me], sem_back, o, across(o))
-        for o in range(1, slices)
-    ]
+    for o in range(1, slices):
+        remote(raw.at[lax.rem(me + o, slices)], back.at[me], sem_back, across(o))
     back[me] = raw[me]
-
     entry_grad = jnp.zeros((lanes, length), F32)
     for r in range(responses):
         proj_c = split(bc_acts[r][0][:, half:])
@@ -379,52 +359,59 @@
         bias_grad,
         jnp.where(column == 1, decay_grad, jnp.where(column == 2, skip_grad, 0.0)),
     )
-    fin[mine, 8 : 8 + heads, 0:half] = head_block
-    fin_copies = fin_copies + send_rows(8, sem_heads)
-
-    for copy in taps_copies:
-        copy.wait_recv()
-    for q in range(groups):
-        total = taps[q * DEV_GROUP, 0:taps_n]
-        for d in range(1, DEV_GROUP):
-            total = total + taps[q * DEV_GROUP + d, 0:taps_n]
-        fin[mine, 16 : 16 + taps_n, q * pair : (q + 1) * pair] = total
-    fin_copies = fin_copies + send_rows(16, sem_fin)
-
-    for copy in back_copies:
-        copy.wait_recv()
+    fin[mine] = jnp.zeros(fin.shape[1:], F32)
+    fin[mine, 0:taps_n, 0:channels] = grad_wx
+    fin[mine, taps_n : taps_n + heads, 0:half] = head_block
+    for o in range(1, peers):
+        remote(fin.at[mine], fin.at[mine], sem_fin, along(o))
+    settle(sem_along, 1, along_taps.at[pl.ds(0, peers - 1)])
+    total = along_taps[0]
+    for z in range(1, peers):
+        total = total + along_taps[z]
+    across_taps[me] = total
+    for o in range(1, slices):
+        remote(across_taps.at[me], across_taps.at[me], sem_across, across(o))
+    settle(sem_back, 1, back.at[pl.ds(0, slices - 1)])
     for q in range(groups):
         total = back[q * DEV_GROUP]
         for d in range(1, DEV_GROUP):
             total = total + back[q * DEV_GROUP + d]
         gbc_ref[:, q * pair : (q + 1) * pair] = total.astype(BF16)
-
-    for copy in fin_copies:
-        copy.wait_recv()
-    for copy in msg_copies + gath_copies + state_copies + taps_copies + back_copies + fin_copies:
-        copy.wait_send()
-
-
-def finish(
-    gx_in, gbc_in, gdt_in, fin, gx_ref, gbc_ref, gdt_ref, gwx_ref, gtaps_ref, gheads_ref, sems
-):
+    settle(sem_fin, 1, fin.at[pl.ds(0, peers - 1)])
+    total = fin[0]
+    for z in range(1, peers):
+        total = total + fin[z]
+    gwx_ref[...] = total[0:taps_n, 0:channels]
+    gheads_ref[...] = total[:, 0:half].T[0:3, taps_n : taps_n + heads]
+
+    for sem, ref in (
+        (sem_msg, msg_out.at[pl.ds(0, peers - 1)]),
+        (sem_gath, gath.at[pl.ds(0, slices - 1)]),
+        (sem_state, state_out.at[pl.ds(0, peers - 1)]),
+        (sem_along, along_taps.at[pl.ds(0, peers - 1)]),
+        (sem_back, raw.at[pl.ds(0, slices - 1)]),
+        (sem_fin, fin.at[pl.ds(0, peers - 1)]),
+    ):
+        settle(sem, 0, ref)
+    settle(sem_across, 1, across_taps.at[pl.ds(0, slices - 1)])
+    for q in range(groups):
+        total = across_taps[q * DEV_GROUP]
+        for d in range(1, DEV_GROUP):
+            total = total + across_taps[q * DEV_GROUP + d]
+        gtaps_ref[:, q * pair : q * pair + half] = total[0:taps_n]
+        gtaps_ref[:, q * pair + half : (q + 1) * pair] = total[taps_n:]
+    settle(sem_across, 0, across_taps.at[pl.ds(0, slices - 1)])
+
+
+def finish(*refs):
+    count = len(refs) // 2
+    sems = refs[-1]
     copies = [
         pltpu.make_async_copy(src, dst, sems.at[i])
-        for i, (src, dst) in enumerate(
-            ((gx_in, gx_ref), (gbc_in, gbc_ref), (gdt_in, gdt_ref))
-        )
+        for i, (src, dst) in enumerate(zip(refs[:count], refs[count:-1]))
     ]
     for copy in copies:
         copy.start()
-    taps_n, channels = gwx_ref.shape
-    heads = gheads_ref.shape[1]
-    pairs = gtaps_ref.shape[1]
-    total = fin[0]
-    for z in range(1, fin.shape[0]):
-        total = total + fin[z]
-    gwx_ref[...] = total[0:taps_n, 0:channels]
-    gtaps_ref[...] = total[16 : 16 + taps_n, 0:pairs]
-    gheads_ref[...] = total[8:16, 0:128].T[0:3, 0:heads]
     for copy in copies:
         copy.wait()
 
@@ -450,7 +437,7 @@
         bc_state = lax.dynamic_slice_in_dim(conv_bc_state, first, pair, 2)
         bc_weight = lax.dynamic_slice_in_dim(conv_bc_weight, first, pair, 1)
     ssm = ssm_state.reshape(prompts, heads * width, nstate)
-    wide = max(all_pairs, channels)
+    rows_fin = -(-(depth + 1 + heads) // 8) * 8
     vmem = pl.BlockSpec(memory_space=pltpu.VMEM)
     dma = pltpu.SemaphoreType.DMA
     outs = (
@@ -461,8 +448,7 @@
         jax.ShapeDtypeStruct((depth + 1, all_pairs), F32),
         jax.ShapeDtypeStruct((3, heads), F32),
     )
-    staged = tuple(pltpu.VMEM(out.shape, out.dtype) for out in outs[:3])
-    staged = staged + (pltpu.VMEM((peers, 24, wide), F32),)
+    staged = tuple(pltpu.VMEM(out.shape, out.dtype) for out in outs)
     args = (
         owner, resp_len, dt_bias, a_log, skip_d, x_raw, bc_raw, dt_raw, cotangent, ssm,
         conv_x_state.transpose(1, 0, 2), bc_state.transpose(1, 0, 2), conv_x_weight, bc_weight,
@@ -471,7 +457,7 @@
         functools.partial(kernel, peers, slices, groups),
         out_shape=staged,
         in_specs=[pl.BlockSpec(memory_space=pltpu.HBM)] * 14,
-        out_specs=[vmem] * 4,
+        out_specs=[vmem] * 6,
         scratch_shapes=[pltpu.SMEM(a.shape, a.dtype) for a in args[:5]]
         + [pltpu.VMEM(a.shape, a.dtype) for a in args[5:]]
         + [
@@ -485,19 +471,14 @@
             pltpu.VMEM((responses, length + 8, channels), F32),
             pltpu.VMEM((responses, length + 8, pair), F32),
             pltpu.VMEM((responses, length, channels), F32),
-            pltpu.VMEM((slices, 8, pair), F32),
             pltpu.VMEM((slices, rows, pair), F32),
             pltpu.VMEM((slices, rows, pair), F32),
+            pltpu.VMEM((peers, rows_fin, max(channels, nstate)), F32),
+            pltpu.VMEM((peers, 2 * depth + 2, nstate), F32),
+            pltpu.VMEM((slices, 2 * depth + 2, nstate), F32),
             dma((14,)),
-            dma((2, peers)),
-            dma((2, peers)),
-            dma((2, slices)),
-            dma((2, slices)),
-            dma((2, slices)),
-            dma((2, peers)),
-            dma((2, peers)),
-            dma((2, peers)),
-        ],
+        ]
+        + [dma((2,))] * 7,
         compiler_params=pltpu.CompilerParams(
             collective_id=0, has_side_effects=True
         ),
@@ -506,9 +487,9 @@
     return pl.pallas_call(
         finish,
         out_shape=outs,
-        in_specs=[vmem] * 4,
-        out_specs=[anywhere] * 3 + [vmem] * 3,
-        scratch_shapes=[dma((3,))],
+        in_specs=[vmem] * 6,
+        out_specs=[anywhere] * 6,
+        scratch_shapes=[dma((6,))],
         compiler_params=pltpu.CompilerParams(vmem_limit_bytes=16 * 1024 * 1024),
     )(*held)
 

time: 23.4 us -> 21.8 us (0.932)
  Pallas kernels: 22.6 us -> 20.9 us
    pallas_call x1, Pallas kernels: 21.3 us -> 20.2 us  [local(): pl.pallas_call(functools.partial(kernel, peers, slices, groups), out_shap...]
    pallas_call x1, Pallas kernels: 1.29 us -> 0.72 us  [local(): pl.pallas_call(finish, out_shape=outs, in_specs=[vmem] * 6, out_specs=[an...]
where the time goes in v1:
time: 21.8 us; the launch traced here: 21.6 us
  Pallas kernels  20.9 us (96%)
  between operations  0.65 us (3%)
    pallas_call x1, Pallas kernels, local(): pl.pallas_call(functools.partial(kernel, peers, slices, groups), out_shap...  20.2 us
    pallas_call x1, Pallas kernels, local(): pl.pallas_call(finish, out_shape=outs, in_specs=[vmem] * 6, out_specs=[an...  0.72 us

profile of v1, /device:TPU:0, one launch (start us, length us, event | category | flops | bytes accessed | tf_op | source)
XLA Modules:
  0.0 21.6 jit_solution(7043927187069925384)
XLA Ops:
  0.6 20.2 %shard_map.181 = (bf16[256,256]{1,0:T(8,128)(2,1)S(1)}, bf16[32,256]{1,0:T(8,128)(2,1)S(1)}, bf16[4,256]{1,0:T(4,128)(2,1)S(1)}, f32[4,256]{1,0:T(4,128)S(1)}, f32[4,256]{1,0:T(4,128)S(1)}, /*index=5*/f32[3,4]{1,0:T(4,128)S(1)}) custom-call(s32[2]{0:T(128)} %refs_0_.1, s32[2]{0:T(128)} %refs_1_.1, f32[4]{0:T(128)} %refs_2_.1, f32[4]{0:T(128)} %refs_3_.1, ...), custom_call_target="tpu_custom_call" | custom-call | tf_op jit(solution)/shard_map/pallas_call | solution.py:456
  20.9 0.7 %shard_map.182 = (bf16[256,256]{1,0:T(8,128)(2,1)}, bf16[32,256]{1,0:T(8,128)(2,1)}, bf16[4,256]{1,0:T(4,128)(2,1)}, f32[4,256]{1,0:T(4,128)}, f32[4,256]{1,0:T(4,128)}, /*index=5*/f32[3,4]{1,0:T(4,128)}) custom-call(bf16[256,256]{1,0:T(8,128)(2,1)S(1)} %get-tuple-element.12.refs_0_, bf16[32,256]{1,0:T(8,128)(2,1)S(1)} %get-tuple-element.13.refs_1_, ...), custom_call_target="tpu_custom_call" | custom-call | tf_op jit(solution)/shard_map/pallas_call | solution.py:487

commit v2 on v1

--- a/solution.py
+++ b/solution.py
@@ -8,6 +8,7 @@
 from jax.sharding import PartitionSpec as P
 
 DEV_GROUP = 8
+FIRST = 2
 GROUP = 1
 MESH = pl.DeviceIdType.MESH
 F32 = jnp.float32
@@ -33,6 +34,10 @@
 
 def iota(shape, dim):
     return lax.broadcasted_iota(jnp.int32, shape, dim)
+
+
+def is_direct(peers, slices, groups):
+    return groups == 1 and peers > 1 and FIRST < slices and peers * slices <= 64
 
 
 def kernel(
@@ -45,7 +50,7 @@
     ssm_ref, cx_ref, cbc_ref, wx_ref, wbc_ref = inputs[9:]
     (
     msg, state, gath, msg_out, state_out, pad_x, pad_bc, dpx, dpbc, dw_ref, raw, back,
-    fin, along_taps, across_taps,
+    fin, all_taps, across_taps, sum_taps, x_act, x_slope, bc_slope, tap_rows, decays, products, score_grads, fed,
     sem_in, sem_msg, sem_state, sem_gath, sem_along, sem_across, sem_back, sem_fin,
     ) = refs
     mine = lax.axis_index("exch")
@@ -65,6 +70,17 @@
 
     def along(offset):
         return {"exch": lax.rem(mine + offset, peers)}
+
+    def spot(place):
+        return {"dp": place % slices, "exch": place // slices}
+
+    def add_up(terms):
+        while len(terms) > 1:
+            terms = [sum(terms[i + 1 : i + 2], terms[i]) for i in range(0, len(terms), 2)]
+        return terms[0]
+
+    devices = peers * slices
+    direct = is_direct(peers, slices, groups)
 
     def across(offset):
         return {"dp": lax.rem(me + offset, slices)}
@@ -174,16 +190,18 @@
     rate = jnp.exp(per_row(a_log))
     first = iota((length, length), 0)
     second = iota((length, length), 1)
-    upto = (first <= second).astype(F32)
-    onward = (first >= second).astype(F32)
+    upto = (first <= second).astype(BF16)
+    onward = (first >= second).astype(BF16)
     causal = first <= second
-    logs = lax.dot_general(
-        -rate * dt,
-        upto,
-        (((1,), (0,)), ((), ())),
-        preferred_element_type=F32,
-        precision=lax.Precision.HIGHEST,
-    )
+
+    def running(rows_in, ones):
+        high = rows_in.astype(BF16).astype(F32)
+        rest = rows_in - high
+        middle = rest.astype(BF16).astype(F32)
+        parts = nn(jnp.concatenate([high, middle, rest - middle], axis=0).astype(BF16), ones)
+        return parts[:lanes] + (parts[lanes : 2 * lanes] + parts[2 * lanes :])
+
+    logs = running(-rate * dt, upto)
     entry = jnp.exp(logs)
     logs_col = logs.T
     dt_col = dt.T
@@ -201,14 +219,40 @@
         head = iota((lanes, channels), 1) // width
         return (row == r * heads + head).astype(BF16)
 
+    wx = wx_ref[...]
+    wbc = wbc_ref[...]
+
+    def convolve(pad, weight, r, count):
+        pre = pad[r, base : base + count] * weight[0:1]
+        for k in range(1, taps_n):
+            pre = pre + pad[r, base + k : base + k + count] * weight[k : k + 1]
+        gate = 1.0 / (1.0 + jnp.exp(-pre))
+        return pre * gate, gate * (1.0 + pre * (1.0 - gate))
+
+    cots, cots_b, dt_fulls = [], [], []
     for r in range(responses):
         block = slice(r * length, (r + 1) * length)
+        pad_x[r, 0:8] = jnp.zeros((8, channels), F32)
         pad_x[r, 8 : 8 + length] = x_ref[block].astype(F32)
-    cots = []
-    for r in range(responses):
-        block = slice(r * length, (r + 1) * length)
         live = iota((length, 1), 0) < lens[r]
         cots.append(jnp.where(live, cot_ref[block].astype(F32), 0.0))
+        cots_b.append(cots[r].astype(BF16))
+        dt_fulls.append(spread_heads(dt_col, r))
+        x_act[r], x_slope[r] = convolve(pad_x, wx, r, length)
+        weighted = split(x_act[r] * dt_fulls[r])
+        total = jnp.zeros((length, length), F32)
+        for h in range(heads):
+            i = r * heads + h
+            cols = slice(h * width, (h + 1) * width)
+            gap = logs[i : i + 1] - logs_col[:, i : i + 1]
+            decay = jnp.where(causal, jnp.exp(jnp.where(causal, gap, 0.0)), 0.0)
+            cot_h = cots_b[r][:, cols]
+            product = (nt(weighted[0][:, cols], cot_h) + nt(weighted[1][:, cols], cot_h)) * decay
+            decays[r, h] = decay
+            products[r, h] = product
+            total = total + product
+        score_grads[r] = total
+        fed[r, 0], fed[r, 1] = split(cots[r] * spread_heads(entry_col, r))
     settle(sem_msg, 1, msg.at[pl.ds(0, peers - 1)])
     got = [msg[z].astype(F32) for z in range(peers)]
     weights = [[None] * peers for _ in range(prompts)]
@@ -225,28 +269,34 @@
         pad_x[r, base:8] = prev[:, :channels]
         pad_bc[r, base:8] = prev[:, channels:]
 
-    def convolve(pad, weight, r):
-        pre = pad[r, base : base + length] * weight[0:1]
-        for k in range(1, taps_n):
-            pre = pre + pad[r, base + k : base + k + length] * weight[k : k + 1]
-        gate = 1.0 / (1.0 + jnp.exp(-pre))
-        return pre * gate, gate * (1.0 + pre * (1.0 - gate))
-
-    wx = wx_ref[...]
-    wbc = wbc_ref[...]
-    x_acts = [convolve(pad_x, wx, r) for r in range(responses)]
+    grads, grads_t = [], []
+    for r in range(responses):
+        act, slope = convolve(pad_x, wx, r, 8)
+        x_act[r, 0:8] = act
+        x_slope[r, 0:8] = slope
+        scaled = act * dt_fulls[r][0:8]
+        high = scaled.astype(BF16).astype(F32)
+        stack = [
+            jnp.where(lane_head == h, part, 0.0)
+            for part in (high, scaled - high)
+            for h in range(heads)
+        ]
+        both = nt(jnp.concatenate(stack, axis=0).astype(BF16), cots_b[r])
+        total = jnp.zeros((8, length), F32)
+        for h in range(heads):
+            lower = 8 * (heads + h)
+            product = (both[8 * h : 8 * h + 8] + both[lower : lower + 8]) * decays[r, h, 0:8]
+            products[r, h, 0:8] = product
+            total = total + product
+        score_grads[r, 0:8] = total
+        whole = score_grads[r]
+        grads.append(split(whole))
+        grads_t.append(split(whole.T))
     settle(sem_gath, 1, gath.at[pl.ds(0, slices - 1)])
     slots = length // rows
     for d in range(slices):
         r, place = d // slots, d % slots
         pad_bc[r, 8 + place * rows : 8 + (place + 1) * rows] = gath[d].astype(F32)
-    bc_acts = [convolve(pad_bc, wbc, r) for r in range(responses)]
-    across_rows = jnp.zeros((lanes, length), F32)
-    dt_first = jnp.zeros((lanes, length), F32)
-    row_index = iota((lanes, 1), 0)
-    skip_sum = jnp.zeros((1, channels), F32)
-    grad_wx = jnp.zeros((taps_n, channels), F32)
-    b_grads, c_grads = [], []
 
     def weight_grad(grad, pad, r):
         parts = [
@@ -261,83 +311,116 @@
             total = total + ref[r, depth - k : depth - k + length] * weight[k : k + 1]
         return total
 
-    for r in range(responses):
-        act, slope = x_acts[r]
-        cot = cots[r]
-        cot_b = cot.astype(BF16)
-        dt_full = spread_heads(dt_col, r)
-        weighted = split(act * dt_full)
-        proj_b = split(bc_acts[r][0][:, :half])
-        proj_c = split(bc_acts[r][0][:, half:])
+    projs = []
+    grad_taps = jnp.zeros((taps_n, pair), F32)
+    for r in range(responses):
+        act, slope = convolve(pad_bc, wbc, r, length)
+        proj_b, proj_c = split(act[:, :half]), split(act[:, half:])
+        projs.append((proj_b, proj_c))
+        b_grad = three(nn, grads[r], proj_c)
+        c_grad = three(nn, grads_t[r], proj_b)
+        pre_grad = jnp.concatenate([b_grad, c_grad], axis=1) * slope
+        dpbc[r, 0:length] = pre_grad
+        dpbc[r, length : length + 8] = jnp.zeros((8, pair), F32)
+        grad_taps = grad_taps + weight_grad(pre_grad, pad_bc, r)
+        bc_slope[r] = slope[:, half:]
+        for k in range(taps_n):
+            window = pad_bc[r, base + k : base + k + length, half:]
+            tap_rows[r, k] = slope[:, half:] * window
+    across_rows = jnp.zeros((lanes, length), F32)
+    dt_first = jnp.zeros((lanes, length), F32)
+    row_index = iota((lanes, 1), 0)
+    skip_sum = jnp.zeros((1, channels), F32)
+    grad_wx = jnp.zeros((taps_n, channels), F32)
+    def local_rows(r, found_rows, dt_rows, skip_row_sum, taps_x):
+        proj_b, proj_c = projs[r]
         scores = three(nt, proj_b, proj_c)
-        score_grad = jnp.zeros((length, length), F32)
         for h in range(heads):
             i = r * heads + h
             cols = slice(h * width, (h + 1) * width)
-            cot_h = cot_b[:, cols]
-            gap = logs[i : i + 1] - logs_col[:, i : i + 1]
-            decay = jnp.where(causal, jnp.exp(jnp.where(causal, gap, 0.0)), 0.0)
-            mix = scores * decay
-            mix_grad = nt(weighted[0][:, cols], cot_h) + nt(weighted[1][:, cols], cot_h)
-            high, low = split(mix)
+            cot_h = cots_b[r][:, cols]
+            high, low = split(scores * decays[r, h])
             dw_ref[r, :, cols] = nn(high, cot_h) + nn(low, cot_h)
-            score_grad = score_grad + mix_grad * decay
-            found = jnp.sum(mix_grad * mix, axis=0, keepdims=True)
-            across_rows = jnp.where(row_index == i, found, across_rows)
-        dw = dw_ref[r]
+            found = jnp.sum(scores * products[r, h], axis=0, keepdims=True)
+            found_rows = jnp.where(row_index == i, found, found_rows)
+        act, dw = x_act[r], dw_ref[r]
         prod = split(dw * act)
         mark = indicator(r)
-        dt_first = dt_first + (nt(mark, prod[0]) + nt(mark, prod[1]))
-        skip_sum = skip_sum + jnp.sum(cot * act, axis=0, keepdims=True)
-        pre_grad = (dw * dt_full + skip_row * cot) * slope
+        dt_rows = dt_rows + (nt(mark, prod[0]) + nt(mark, prod[1]))
+        skip_row_sum = skip_row_sum + jnp.sum(cots[r] * act, axis=0, keepdims=True)
+        pre_grad = (dw * dt_fulls[r] + skip_row * cots[r]) * x_slope[r]
         dpx[r, 0:length] = pre_grad
         dpx[r, length : length + 8] = jnp.zeros((8, channels), F32)
-        grad_wx = grad_wx + weight_grad(pre_grad, pad_x, r)
+        taps_x = taps_x + weight_grad(pre_grad, pad_x, r)
         gx_ref[r * length : (r + 1) * length] = input_grad(dpx, wx, r).astype(BF16)
-        b_grads.append(three(nn, split(score_grad), proj_c))
-        c_grads.append(three(nn, split(score_grad.T), proj_b))
+        return found_rows, dt_rows, skip_row_sum, taps_x
+
+    sums = (across_rows, dt_first, skip_sum, grad_wx)
+    early = responses
+    for r in range(early):
+        sums = local_rows(r, *sums)
     settle(sem_state, 1, state.at[pl.ds(0, peers - 1)])
-    starts = []
-    grad_taps = jnp.zeros((taps_n, pair), F32)
-    for r in range(responses):
-        start = jnp.zeros(state.shape[1:], F32)
+    starts, lates = [], []
+    for r in range(responses):
+        start = jnp.zeros(state.shape[1:], BF16)
         for z in range(peers):
-            pick = weights[r // GROUP][z][:, : state.shape[2]]
-            start = start + state[z].astype(F32) * pick
-        start = start.astype(BF16)
+            pick = weights[r // GROUP][z][:, : state.shape[2]].astype(BF16)
+            start = start + state[z] * pick
         starts.append(start)
-        fed = split(cots[r] * spread_heads(entry_col, r))
-        c_grad = c_grads[r] + (nn(fed[0], start) + nn(fed[1], start))
-        slope = bc_acts[r][1]
-        pre_grad = jnp.concatenate([b_grads[r], c_grad], axis=1) * slope
-        dpbc[r, 0:length] = pre_grad
-        dpbc[r, length : length + 8] = jnp.zeros((8, pair), F32)
-        grad_taps = grad_taps + weight_grad(pre_grad, pad_bc, r)
-    along_taps[mine] = jnp.concatenate([grad_taps[:, :half], grad_taps[:, half:]], axis=0)
-    for o in range(1, peers):
-        remote(along_taps.at[mine], along_taps.at[mine], sem_along, along(o))
-    for r in range(responses):
+        late = nn(fed[r, 0], start) + nn(fed[r, 1], start)
+        lates.append(late)
+        more = jnp.concatenate(
+            [jnp.sum(late * tap_rows[r, k], axis=0, keepdims=True) for k in range(taps_n)], axis=0
+        )
+        grad_taps = grad_taps + jnp.concatenate([jnp.zeros_like(more), more], axis=1)
+    packed = jnp.concatenate([grad_taps[:, :half], grad_taps[:, half:]], axis=0)
+    if direct:
+        place = mine * slices + me
+        helper = slices + 1
+        is_helper = place == helper
+        is_first = place < FIRST
+        all_taps[place] = packed
+        for target in (*range(FIRST), helper):
+
+            @pl.when(place != target)
+            def _():
+                remote(all_taps.at[place], all_taps.at[place], sem_along, spot(target))
+
+        def sum_all():
+            settle(sem_along, 1, all_taps.at[pl.ds(0, devices - 1)])
+            for q in range(groups):
+                sum_taps[q] = add_up(
+                    [
+                        all_taps[z * slices + q * DEV_GROUP + d]
+                        for z in range(peers)
+                        for d in range(DEV_GROUP)
+                    ]
+                )
+
+    else:
+        all_taps[mine] = packed
+        for o in range(1, peers):
+            remote(all_taps.at[mine], all_taps.at[mine], sem_along, along(o))
+    for r in range(responses):
+        dpbc[r, 0:length, half:] = dpbc[r, 0:length, half:] + lates[r] * bc_slope[r]
         block = input_grad(dpbc, wbc, r)
         for place in range(slots):
             raw[r * slots + place] = block[place * rows : (place + 1) * rows]
     for o in range(1, slices):
         remote(raw.at[lax.rem(me + o, slices)], back.at[me], sem_back, across(o))
     back[me] = raw[me]
+    for r in range(early, responses):
+        sums = local_rows(r, *sums)
+    across_rows, dt_first, skip_sum, grad_wx = sums
     entry_grad = jnp.zeros((lanes, length), F32)
     for r in range(responses):
-        proj_c = split(bc_acts[r][0][:, half:])
+        proj_c = projs[r][1]
         carried = nt(proj_c[0], starts[r]) + nt(proj_c[1], starts[r])
         prod = split(carried * cots[r])
         mark = indicator(r)
         entry_grad = entry_grad + (nt(mark, prod[0]) + nt(mark, prod[1]))
     log_grad = across_rows + entry * entry_grad - dt * dt_first
-    step_grad = lax.dot_general(
-        log_grad,
-        onward,
-        (((1,), (0,)), ((), ())),
-        preferred_element_type=F32,
-        precision=lax.Precision.HIGHEST,
-    )
+    step_grad = running(log_grad, onward)
     dt_grad = dt_first - rate * step_grad
     raw_grad = dt_grad * (1.0 / (1.0 + jnp.exp(-dt_pre)))
     for r in range(responses):
@@ -353,24 +436,27 @@
         decay_grad = decay_grad + decay_rows[r * heads : (r + 1) * heads]
     own = iota((heads, channels), 0) == iota((heads, channels), 1) // width
     skip_grad = jnp.sum(jnp.where(own, skip_sum, 0.0), axis=1, keepdims=True)
-    column = iota((heads, half), 1)
-    head_block = jnp.where(
-        column == 0,
-        bias_grad,
-        jnp.where(column == 1, decay_grad, jnp.where(column == 2, skip_grad, 0.0)),
-    )
+    at_head = iota((heads, half), 0) == iota((heads, half), 1)
     fin[mine] = jnp.zeros(fin.shape[1:], F32)
     fin[mine, 0:taps_n, 0:channels] = grad_wx
-    fin[mine, taps_n : taps_n + heads, 0:half] = head_block
+    for i, grad in enumerate((bias_grad, decay_grad, skip_grad)):
+        row = jnp.sum(jnp.where(at_head, grad, 0.0), axis=0, keepdims=True)
+        fin[mine, taps_n + i : taps_n + i + 1, 0:half] = row
     for o in range(1, peers):
         remote(fin.at[mine], fin.at[mine], sem_fin, along(o))
-    settle(sem_along, 1, along_taps.at[pl.ds(0, peers - 1)])
-    total = along_taps[0]
-    for z in range(1, peers):
-        total = total + along_taps[z]
-    across_taps[me] = total
-    for o in range(1, slices):
-        remote(across_taps.at[me], across_taps.at[me], sem_across, across(o))
+    if direct:
+
+        @pl.when(is_helper)
+        def _():
+            sum_all()
+            for k in range(FIRST, devices):
+                if k != helper:
+                    remote(sum_taps, sum_taps, sem_across, spot(k))
+    else:
+        settle(sem_along, 1, all_taps.at[pl.ds(0, peers - 1)])
+        across_taps[me] = add_up([all_taps[z] for z in range(peers)])
+        for o in range(1, slices):
+            remote(across_taps.at[me], across_taps.at[me], sem_across, across(o))
     settle(sem_back, 1, back.at[pl.ds(0, slices - 1)])
     for q in range(groups):
         total = back[q * DEV_GROUP]
@@ -382,25 +468,42 @@
     for z in range(1, peers):
         total = total + fin[z]
     gwx_ref[...] = total[0:taps_n, 0:channels]
-    gheads_ref[...] = total[:, 0:half].T[0:3, taps_n : taps_n + heads]
+    gheads_ref[...] = total[taps_n : taps_n + 3, 0:heads]
 
     for sem, ref in (
         (sem_msg, msg_out.at[pl.ds(0, peers - 1)]),
         (sem_gath, gath.at[pl.ds(0, slices - 1)]),
         (sem_state, state_out.at[pl.ds(0, peers - 1)]),
-        (sem_along, along_taps.at[pl.ds(0, peers - 1)]),
         (sem_back, raw.at[pl.ds(0, slices - 1)]),
         (sem_fin, fin.at[pl.ds(0, peers - 1)]),
     ):
         settle(sem, 0, ref)
-    settle(sem_across, 1, across_taps.at[pl.ds(0, slices - 1)])
+    if direct:
+
+        @pl.when(is_helper)
+        def _():
+            settle(sem_along, 0, all_taps.at[pl.ds(0, FIRST)])
+            settle(sem_across, 0, all_taps.at[pl.ds(0, (devices - 1 - FIRST) * groups)])
+
+        @pl.when(is_first)
+        def _():
+            settle(sem_along, 0, all_taps.at[pl.ds(0, FIRST)])
+            sum_all()
+
+        @pl.when(jnp.logical_not(jnp.logical_or(is_first, is_helper)))
+        def _():
+            settle(sem_along, 0, all_taps.at[pl.ds(0, FIRST + 1)])
+            settle(sem_across, 1, sum_taps)
+    else:
+        settle(sem_along, 0, all_taps.at[pl.ds(0, peers - 1)])
+        settle(sem_across, 0, across_taps.at[pl.ds(0, slices - 1)])
+        settle(sem_across, 1, across_taps.at[pl.ds(0, slices - 1)])
+        for q in range(groups):
+            sum_taps[q] = add_up([across_taps[q * DEV_GROUP + d] for d in range(DEV_GROUP)])
     for q in range(groups):
-        total = across_taps[q * DEV_GROUP]
-        for d in range(1, DEV_GROUP):
-            total = total + across_taps[q * DEV_GROUP + d]
+        total = sum_taps[q]
         gtaps_ref[:, q * pair : q * pair + half] = total[0:taps_n]
         gtaps_ref[:, q * pair + half : (q + 1) * pair] = total[taps_n:]
-    settle(sem_across, 0, across_taps.at[pl.ds(0, slices - 1)])
 
 
 def finish(*refs):
@@ -437,7 +540,8 @@
         bc_state = lax.dynamic_slice_in_dim(conv_bc_state, first, pair, 2)
         bc_weight = lax.dynamic_slice_in_dim(conv_bc_weight, first, pair, 1)
     ssm = ssm_state.reshape(prompts, heads * width, nstate)
-    rows_fin = -(-(depth + 1 + heads) // 8) * 8
+    senders = peers * slices if is_direct(peers, slices, groups) else peers
+    rows_fin = -(-(depth + 4) // 8) * 8
     vmem = pl.BlockSpec(memory_space=pltpu.VMEM)
     dma = pltpu.SemaphoreType.DMA
     outs = (
@@ -474,8 +578,17 @@
             pltpu.VMEM((slices, rows, pair), F32),
             pltpu.VMEM((slices, rows, pair), F32),
             pltpu.VMEM((peers, rows_fin, max(channels, nstate)), F32),
-            pltpu.VMEM((peers, 2 * depth + 2, nstate), F32),
+            pltpu.VMEM((senders, 2 * depth + 2, nstate), F32),
             pltpu.VMEM((slices, 2 * depth + 2, nstate), F32),
+            pltpu.VMEM((groups, 2 * depth + 2, nstate), F32),
+            pltpu.VMEM((responses, length, channels), F32),
+            pltpu.VMEM((responses, length, channels), F32),
+            pltpu.VMEM((responses, length, nstate), F32),
+            pltpu.VMEM((responses, depth + 1, length, nstate), F32),
+            pltpu.VMEM((responses, heads, length, length), F32),
+            pltpu.VMEM((responses, heads, length, length), F32),
+            pltpu.VMEM((responses, length, length), F32),
+            pltpu.VMEM((responses, 2, length, channels), BF16),
             dma((14,)),
         ]
         + [dma((2,))] * 7,

time: 21.8 us -> 19.6 us (0.90)
  the two profiles are of different devices: /device:TPU:0 before, /device:TPU:7 now
where the time goes in v2:
time: 19.6 us; the launch traced here: 19.4 us
  Pallas kernels  18.7 us (95%)
  between operations  0.65 us (3%)
    pallas_call x1, Pallas kernels, local(): pl.pallas_call(functools.partial(kernel, peers, slices, groups), out_shap...  18 us
    pallas_call x1, Pallas kernels, local(): pl.pallas_call(finish, out_shape=outs, in_specs=[vmem] * 6, out_specs=[an...  0.72 us

profile of v2, /device:TPU:7, one launch (start us, length us, event | category | flops | bytes accessed | tf_op | source)
XLA Modules:
  0.0 19.4 jit_solution(12842265894129148811)
XLA Ops:
  0.6 18.0 %shard_map.181 = (bf16[256,256]{1,0:T(8,128)(2,1)S(1)}, bf16[32,256]{1,0:T(8,128)(2,1)S(1)}, bf16[4,256]{1,0:T(4,128)(2,1)S(1)}, f32[4,256]{1,0:T(4,128)S(1)}, f32[4,256]{1,0:T(4,128)S(1)}, /*index=5*/f32[3,4]{1,0:T(4,128)S(1)}) custom-call(s32[2]{0:T(128)} %refs_0_.1, s32[2]{0:T(128)} %refs_1_.1, f32[4]{0:T(128)} %refs_2_.1, f32[4]{0:T(128)} %refs_3_.1, ...), custom_call_target="tpu_custom_call" | custom-call | tf_op jit(solution)/shard_map/pallas_call | solution.py:560
  18.6 0.7 %shard_map.182 = (bf16[256,256]{1,0:T(8,128)(2,1)}, bf16[32,256]{1,0:T(8,128)(2,1)}, bf16[4,256]{1,0:T(4,128)(2,1)}, f32[4,256]{1,0:T(4,128)}, f32[4,256]{1,0:T(4,128)}, /*index=5*/f32[3,4]{1,0:T(4,128)}) custom-call(bf16[256,256]{1,0:T(8,128)(2,1)S(1)} %get-tuple-element.12.refs_0_, bf16[32,256]{1,0:T(8,128)(2,1)S(1)} %get-tuple-element.13.refs_1_, ...), custom_call_target="tpu_custom_call" | custom-call | tf_op jit(solution)/shard_map/pallas_call | solution.py:600

commit v3 on v2

--- a/solution.py
+++ b/solution.py
@@ -8,7 +8,7 @@
 from jax.sharding import PartitionSpec as P
 
 DEV_GROUP = 8
-FIRST = 2
+AHEAD = 1
 GROUP = 1
 MESH = pl.DeviceIdType.MESH
 F32 = jnp.float32
@@ -28,8 +28,14 @@
     return high, (a - high.astype(F32)).astype(BF16)
 
 
+def two(dot, a, b):
+    rows = a[0].shape[0]
+    both = dot(jnp.concatenate(a, axis=0), b)
+    return both[:rows] + both[rows:]
+
+
 def three(dot, a, b):
-    return dot(a[0], b[0]) + (dot(a[0], b[1]) + dot(a[1], b[0]))
+    return two(dot, a, b[0]) + dot(a[0], b[1])
 
 
 def iota(shape, dim):
@@ -37,7 +43,7 @@
 
 
 def is_direct(peers, slices, groups):
-    return groups == 1 and peers > 1 and FIRST < slices and peers * slices <= 64
+    return groups == 1 and peers > 1 and peers * slices <= 64
 
 
 def kernel(
@@ -51,7 +57,8 @@
     (
     msg, state, gath, msg_out, state_out, pad_x, pad_bc, dpx, dpbc, dw_ref, raw, back,
     fin, all_taps, across_taps, sum_taps, x_act, x_slope, bc_slope, tap_rows, decays, products, score_grads, fed,
-    sem_in, sem_msg, sem_state, sem_gath, sem_along, sem_across, sem_back, sem_fin,
+    taken, sent,
+    sem_in, sem_out, sem_msg, sem_state, sem_gath, sem_back, sem_fin, sem_along, sem_across,
     ) = refs
     mine = lax.axis_index("exch")
     me = lax.axis_index("dp")
@@ -90,15 +97,14 @@
         pl.semaphore_signal(barrier, inc=1, device_id=along(offset), device_id_type=MESH)
     for offset in range(1, slices):
         pl.semaphore_signal(barrier, inc=1, device_id=across(offset), device_id_type=MESH)
+    sooner, later, blocks = (6, 0, 10, 11, 9), (1, 2, 3, 4), (5, 7, 8, 12, 13)
     loads = [
-        pltpu.make_async_copy(src, dst, sem_in.at[i])
+        pltpu.make_async_copy(src, dst, sem_in.at[0 if i in blocks else 1 + (sooner + later).index(i)])
         for i, (src, dst) in enumerate(zip(sources, inputs))
     ]
-    sooner = (6, 0, 10, 11, 9)
-    later = [i for i in range(len(loads)) if i not in sooner]
     for i in sooner:
         loads[i].start()
-    for i in later:
+    for i in later + blocks:
         loads[i].start()
     for i in sooner[:-1]:
         loads[i].wait()
@@ -136,11 +142,12 @@
     fill_msg(mine, msg.at[mine])
     pl.semaphore_wait(barrier, slices - 1 + peers - 1)
     def remote(src, dst, sem, where):
+        shared = sem.shape[0] == 1
         pltpu.make_async_remote_copy(
             src_ref=src,
             dst_ref=dst,
-            send_sem=sem.at[0],
-            recv_sem=sem.at[1],
+            send_sem=sem_out.at[0] if shared else sem.at[0],
+            recv_sem=sem.at[0] if shared else sem.at[1],
             device_id=where,
             device_id_type=MESH,
         ).start()
@@ -162,11 +169,19 @@
     loads[sooner[-1]].wait()
     for k in range(peers - 1):
         fill_state(order[k], state_out.at[k])
-        remote(state_out.at[k], state.at[mine], sem_state, {"exch": order[k]})
+        if k < AHEAD:
+            remote(state_out.at[k], state.at[mine], sem_state, {"exch": order[k]})
     fill_state(mine, state.at[mine])
+
+    def send_states():
+        for k in range(AHEAD, peers - 1):
+            remote(state_out.at[k], state.at[mine], sem_state, {"exch": order[k]})
+
+    pl.when(lax.rem(me, 2) == 0)(send_states)
     gath[me] = group_columns(bc_ref, me)[...]
     for i in later:
         loads[i].wait()
+    settle(sem_in, 0, taken)
     row_head = lax.rem(iota((lanes, 1), 0), heads)
 
     def per_row(ref):
@@ -223,11 +238,12 @@
     wbc = wbc_ref[...]
 
     def convolve(pad, weight, r, count):
-        pre = pad[r, base : base + count] * weight[0:1]
+        windows = [pad[r, base + k : base + k + count] for k in range(taps_n)]
+        pre = windows[0] * weight[0:1]
         for k in range(1, taps_n):
-            pre = pre + pad[r, base + k : base + k + count] * weight[k : k + 1]
+            pre = pre + windows[k] * weight[k : k + 1]
         gate = 1.0 / (1.0 + jnp.exp(-pre))
-        return pre * gate, gate * (1.0 + pre * (1.0 - gate))
+        return pre * gate, gate * (1.0 + pre * (1.0 - gate)), windows
 
     cots, cots_b, dt_fulls = [], [], []
     for r in range(responses):
@@ -238,7 +254,7 @@
         cots.append(jnp.where(live, cot_ref[block].astype(F32), 0.0))
         cots_b.append(cots[r].astype(BF16))
         dt_fulls.append(spread_heads(dt_col, r))
-        x_act[r], x_slope[r] = convolve(pad_x, wx, r, length)
+        x_act[r], x_slope[r], _ = convolve(pad_x, wx, r, length)
         weighted = split(x_act[r] * dt_fulls[r])
         total = jnp.zeros((length, length), F32)
         for h in range(heads):
@@ -247,13 +263,13 @@
             gap = logs[i : i + 1] - logs_col[:, i : i + 1]
             decay = jnp.where(causal, jnp.exp(jnp.where(causal, gap, 0.0)), 0.0)
             cot_h = cots_b[r][:, cols]
-            product = (nt(weighted[0][:, cols], cot_h) + nt(weighted[1][:, cols], cot_h)) * decay
+            product = two(nt, [part[:, cols] for part in weighted], cot_h) * decay
             decays[r, h] = decay
             products[r, h] = product
             total = total + product
         score_grads[r] = total
-        fed[r, 0], fed[r, 1] = split(cots[r] * spread_heads(entry_col, r))
-    settle(sem_msg, 1, msg.at[pl.ds(0, peers - 1)])
+        fed[r, 0:length], fed[r, length:] = split(cots[r] * spread_heads(entry_col, r))
+    settle(sem_msg, 0, msg.at[pl.ds(0, peers - 1)])
     got = [msg[z].astype(F32) for z in range(peers)]
     weights = [[None] * peers for _ in range(prompts)]
     seen = jnp.zeros((1, channels + pair), F32)
@@ -271,7 +287,7 @@
 
     grads, grads_t = [], []
     for r in range(responses):
-        act, slope = convolve(pad_x, wx, r, 8)
+        act, slope, _ = convolve(pad_x, wx, r, 8)
         x_act[r, 0:8] = act
         x_slope[r, 0:8] = slope
         scaled = act * dt_fulls[r][0:8]
@@ -292,41 +308,90 @@
         whole = score_grads[r]
         grads.append(split(whole))
         grads_t.append(split(whole.T))
-    settle(sem_gath, 1, gath.at[pl.ds(0, slices - 1)])
+    settle(sem_gath, 0, gath.at[pl.ds(0, slices - 1)])
     slots = length // rows
     for d in range(slices):
         r, place = d // slots, d % slots
         pad_bc[r, 8 + place * rows : 8 + (place + 1) * rows] = gath[d].astype(F32)
 
-    def weight_grad(grad, pad, r):
-        parts = [
-            jnp.sum(grad * pad[r, base + k : base + k + length], axis=0, keepdims=True)
-            for k in range(taps_n)
-        ]
+    def tap_sums(grad, windows):
+        parts = [jnp.sum(grad * window, axis=0, keepdims=True) for window in windows]
         return jnp.concatenate(parts, axis=0)
 
-    def input_grad(ref, weight, r):
-        total = ref[r, depth : depth + length] * weight[0:1]
-        for k in range(1, taps_n):
-            total = total + ref[r, depth - k : depth - k + length] * weight[k : k + 1]
+    def input_grad(windows, weight, cols):
+        total = windows[0] * weight[depth : depth + 1, cols]
+        for j in range(1, taps_n):
+            total = total + windows[j] * weight[depth - j : taps_n - j, cols]
         return total
 
+    def send_bc(part):
+        for r in range(responses):
+            cols = slice(part * half, (part + 1) * half)
+            block = input_grad([dpbc[r, j : j + length, cols] for j in range(taps_n)], wbc, cols)
+            for place in range(slots):
+                raw[part, r * slots + place] = block[place * rows : (place + 1) * rows]
+        for o in range(1, slices):
+            remote(raw.at[part, lax.rem(me + o, slices)], back.at[part, me], sem_back, across(o))
+        back[part, me] = raw[part, me]
+
     projs = []
-    grad_taps = jnp.zeros((taps_n, pair), F32)
-    for r in range(responses):
-        act, slope = convolve(pad_bc, wbc, r, length)
+    b_taps = jnp.zeros((taps_n, half), F32)
+    c_taps = jnp.zeros((taps_n, half), F32)
+    for r in range(responses):
+        act, slope, windows = convolve(pad_bc, wbc, r, length)
         proj_b, proj_c = split(act[:, :half]), split(act[:, half:])
         projs.append((proj_b, proj_c))
-        b_grad = three(nn, grads[r], proj_c)
+        pre_grad = three(nn, grads[r], proj_c) * slope[:, :half]
         c_grad = three(nn, grads_t[r], proj_b)
-        pre_grad = jnp.concatenate([b_grad, c_grad], axis=1) * slope
-        dpbc[r, 0:length] = pre_grad
+        dpbc[r, 0:length, 0:half] = pre_grad
+        dpbc[r, 0:length, half:] = c_grad
         dpbc[r, length : length + 8] = jnp.zeros((8, pair), F32)
-        grad_taps = grad_taps + weight_grad(pre_grad, pad_bc, r)
         bc_slope[r] = slope[:, half:]
         for k in range(taps_n):
-            window = pad_bc[r, base + k : base + k + length, half:]
-            tap_rows[r, k] = slope[:, half:] * window
+            tap_rows[r, k] = slope[:, half:] * windows[k][:, half:]
+        b_taps = b_taps + tap_sums(pre_grad, [window[:, :half] for window in windows])
+        c_taps = c_taps + tap_sums(c_grad, [tap_rows[r, k] for k in range(taps_n)])
+
+    place = mine * slices + me
+    helper = slices + slices // 2 + 1
+    is_helper = place == helper
+    is_first = mine == 0
+    slot = place if direct else mine
+
+    def send_taps(part, value):
+        all_taps[part, slot] = value
+        block = all_taps.at[part, slot]
+        if not direct:
+            for o in range(1, peers):
+                remote(block, block, sem_along, along(o))
+            return
+        for target in (0, 1, helper, *range(2, slices)):
+
+            @pl.when(place != target)
+            def _():
+                remote(block, block, sem_along, spot(target))
+
+    def sum_all():
+        settle(sem_along, 1, all_taps.at[:, pl.ds(0, devices - 1)])
+        for q in range(groups):
+            sum_taps[q] = jnp.concatenate(
+                [
+                    add_up(
+                        [
+                            all_taps[part, z * slices + q * DEV_GROUP + d]
+                            for z in range(peers)
+                            for d in range(DEV_GROUP)
+                        ]
+                    )
+                    for part in range(2)
+                ],
+                axis=0,
+            )
+
+    send_taps(0, b_taps)
+    send_bc(0)
+
+    pl.when(lax.rem(me, 2) == 1)(send_states)
     across_rows = jnp.zeros((lanes, length), F32)
     dt_first = jnp.zeros((lanes, length), F32)
     row_index = iota((lanes, 1), 0)
@@ -339,8 +404,7 @@
             i = r * heads + h
             cols = slice(h * width, (h + 1) * width)
             cot_h = cots_b[r][:, cols]
-            high, low = split(scores * decays[r, h])
-            dw_ref[r, :, cols] = nn(high, cot_h) + nn(low, cot_h)
+            dw_ref[r, :, cols] = two(nn, split(scores * decays[r, h]), cot_h)
             found = jnp.sum(scores * products[r, h], axis=0, keepdims=True)
             found_rows = jnp.where(row_index == i, found, found_rows)
         act, dw = x_act[r], dw_ref[r]
@@ -351,15 +415,24 @@
         pre_grad = (dw * dt_fulls[r] + skip_row * cots[r]) * x_slope[r]
         dpx[r, 0:length] = pre_grad
         dpx[r, length : length + 8] = jnp.zeros((8, channels), F32)
-        taps_x = taps_x + weight_grad(pre_grad, pad_x, r)
-        gx_ref[r * length : (r + 1) * length] = input_grad(dpx, wx, r).astype(BF16)
+        windows = [pre_grad] + [dpx[r, j : j + length] for j in range(1, taps_n)]
+        block = input_grad(windows, wx, slice(0, channels))
+        gx_ref[r * length : (r + 1) * length] = block.astype(BF16)
+        raw_x = pad_x[r, 8 : 8 + length]
+        parts = []
+        for j in range(depth, -1, -1):
+            part = jnp.sum(windows[j] * raw_x, axis=0, keepdims=True)
+            if j > 0:
+                edge = dpx[r, 0:j] * pad_x[r, 8 - j : 8]
+                part = part + jnp.sum(edge, axis=0, keepdims=True)
+            parts.append(part)
+        taps_x = taps_x + jnp.concatenate(parts, axis=0)
         return found_rows, dt_rows, skip_row_sum, taps_x
 
     sums = (across_rows, dt_first, skip_sum, grad_wx)
-    early = responses
-    for r in range(early):
+    for r in range(responses):
         sums = local_rows(r, *sums)
-    settle(sem_state, 1, state.at[pl.ds(0, peers - 1)])
+    settle(sem_state, 0, state.at[pl.ds(0, peers - 1)])
     starts, lates = [], []
     for r in range(responses):
         start = jnp.zeros(state.shape[1:], BF16)
@@ -367,55 +440,16 @@
             pick = weights[r // GROUP][z][:, : state.shape[2]].astype(BF16)
             start = start + state[z] * pick
         starts.append(start)
-        late = nn(fed[r, 0], start) + nn(fed[r, 1], start)
+        both = nn(fed[r], start)
+        late = both[:length] + both[length:]
         lates.append(late)
-        more = jnp.concatenate(
-            [jnp.sum(late * tap_rows[r, k], axis=0, keepdims=True) for k in range(taps_n)], axis=0
-        )
-        grad_taps = grad_taps + jnp.concatenate([jnp.zeros_like(more), more], axis=1)
-    packed = jnp.concatenate([grad_taps[:, :half], grad_taps[:, half:]], axis=0)
-    if direct:
-        place = mine * slices + me
-        helper = slices + 1
-        is_helper = place == helper
-        is_first = place < FIRST
-        all_taps[place] = packed
-        for target in (*range(FIRST), helper):
-
-            @pl.when(place != target)
-            def _():
-                remote(all_taps.at[place], all_taps.at[place], sem_along, spot(target))
-
-        def sum_all():
-            settle(sem_along, 1, all_taps.at[pl.ds(0, devices - 1)])
-            for q in range(groups):
-                sum_taps[q] = add_up(
-                    [
-                        all_taps[z * slices + q * DEV_GROUP + d]
-                        for z in range(peers)
-                        for d in range(DEV_GROUP)
-                    ]
-                )
-
-    else:
-        all_taps[mine] = packed
-        for o in range(1, peers):
-            remote(all_taps.at[mine], all_taps.at[mine], sem_along, along(o))
-    for r in range(responses):
-        dpbc[r, 0:length, half:] = dpbc[r, 0:length, half:] + lates[r] * bc_slope[r]
-        block = input_grad(dpbc, wbc, r)
-        for place in range(slots):
-            raw[r * slots + place] = block[place * rows : (place + 1) * rows]
-    for o in range(1, slices):
-        remote(raw.at[lax.rem(me + o, slices)], back.at[me], sem_back, across(o))
-    back[me] = raw[me]
-    for r in range(early, responses):
-        sums = local_rows(r, *sums)
+        c_taps = c_taps + tap_sums(late, [tap_rows[r, k] for k in range(taps_n)])
+    send_taps(1, c_taps)
     across_rows, dt_first, skip_sum, grad_wx = sums
     entry_grad = jnp.zeros((lanes, length), F32)
     for r in range(responses):
         proj_c = projs[r][1]
-        carried = nt(proj_c[0], starts[r]) + nt(proj_c[1], starts[r])
+        carried = two(nt, proj_c, starts[r])
         prod = split(carried * cots[r])
         mark = indicator(r)
         entry_grad = entry_grad + (nt(mark, prod[0]) + nt(mark, prod[1]))
@@ -444,58 +478,57 @@
         fin[mine, taps_n + i : taps_n + i + 1, 0:half] = row
     for o in range(1, peers):
         remote(fin.at[mine], fin.at[mine], sem_fin, along(o))
+
+    for r in range(responses):
+        dpbc[r, 0:length, half:] = (dpbc[r, 0:length, half:] + lates[r]) * bc_slope[r]
+    send_bc(1)
     if direct:
 
         @pl.when(is_helper)
         def _():
             sum_all()
-            for k in range(FIRST, devices):
+            for k in range(slices, devices):
                 if k != helper:
                     remote(sum_taps, sum_taps, sem_across, spot(k))
     else:
-        settle(sem_along, 1, all_taps.at[pl.ds(0, peers - 1)])
-        across_taps[me] = add_up([all_taps[z] for z in range(peers)])
+        settle(sem_along, 1, all_taps.at[:, pl.ds(0, peers - 1)])
+        across_taps[me] = jnp.concatenate(
+            [add_up([all_taps[part, z] for z in range(peers)]) for part in range(2)], axis=0
+        )
         for o in range(1, slices):
             remote(across_taps.at[me], across_taps.at[me], sem_across, across(o))
-    settle(sem_back, 1, back.at[pl.ds(0, slices - 1)])
+    settle(sem_back, 0, back.at[:, pl.ds(0, slices - 1)])
     for q in range(groups):
-        total = back[q * DEV_GROUP]
-        for d in range(1, DEV_GROUP):
-            total = total + back[q * DEV_GROUP + d]
-        gbc_ref[:, q * pair : (q + 1) * pair] = total.astype(BF16)
-    settle(sem_fin, 1, fin.at[pl.ds(0, peers - 1)])
+        for part in range(2):
+            total = add_up([back[part, q * DEV_GROUP + d] for d in range(DEV_GROUP)])
+            first_col = q * pair + part * half
+            gbc_ref[:, first_col : first_col + half] = total.astype(BF16)
+    settle(sem_fin, 0, fin.at[pl.ds(0, peers - 1)])
     total = fin[0]
     for z in range(1, peers):
         total = total + fin[z]
     gwx_ref[...] = total[0:taps_n, 0:channels]
     gheads_ref[...] = total[taps_n : taps_n + 3, 0:heads]
 
-    for sem, ref in (
-        (sem_msg, msg_out.at[pl.ds(0, peers - 1)]),
-        (sem_gath, gath.at[pl.ds(0, slices - 1)]),
-        (sem_state, state_out.at[pl.ds(0, peers - 1)]),
-        (sem_back, raw.at[pl.ds(0, slices - 1)]),
-        (sem_fin, fin.at[pl.ds(0, peers - 1)]),
-    ):
-        settle(sem, 0, ref)
+    settle(sem_out, 0, sent)
     if direct:
 
         @pl.when(is_helper)
         def _():
-            settle(sem_along, 0, all_taps.at[pl.ds(0, FIRST)])
-            settle(sem_across, 0, all_taps.at[pl.ds(0, (devices - 1 - FIRST) * groups)])
+            settle(sem_along, 0, all_taps.at[:, pl.ds(0, slices)])
+            settle(sem_across, 0, all_taps.at[:, pl.ds(0, devices - 1 - slices)])
 
         @pl.when(is_first)
         def _():
-            settle(sem_along, 0, all_taps.at[pl.ds(0, FIRST)])
+            settle(sem_along, 0, all_taps.at[:, pl.ds(0, slices)])
             sum_all()
 
         @pl.when(jnp.logical_not(jnp.logical_or(is_first, is_helper)))
         def _():
-            settle(sem_along, 0, all_taps.at[pl.ds(0, FIRST + 1)])
+            settle(sem_along, 0, all_taps.at[:, pl.ds(0, slices + 1)])
             settle(sem_across, 1, sum_taps)
     else:
-        settle(sem_along, 0, all_taps.at[pl.ds(0, peers - 1)])
+        settle(sem_along, 0, all_taps.at[:, pl.ds(0, peers - 1)])
         settle(sem_across, 0, across_taps.at[pl.ds(0, slices - 1)])
         settle(sem_across, 1, across_taps.at[pl.ds(0, slices - 1)])
         for q in range(groups):
@@ -557,6 +590,12 @@
         owner, resp_len, dt_bias, a_log, skip_d, x_raw, bc_raw, dt_raw, cotangent, ssm,
         conv_x_state.transpose(1, 0, 2), bc_state.transpose(1, 0, 2), conv_x_weight, bc_weight,
     )
+    taken = sum(args[i].size * args[i].dtype.itemsize for i in (5, 7, 8, 12, 13))
+    row = 4 * pair
+    sent = (peers - 1) * (2 * (depth + 1) * (channels + pair) + 2 * heads * width * nstate)
+    sent = sent + (peers - 1) * 4 * rows_fin * max(channels, nstate)
+    sent = sent + (slices - 1) * (rows * row // 2 + rows * row)
+    assert taken % 2048 == 0 and sent % 2048 == 0
     held = pl.pallas_call(
         functools.partial(kernel, peers, slices, groups),
         out_shape=staged,
@@ -575,10 +614,10 @@
             pltpu.VMEM((responses, length + 8, channels), F32),
             pltpu.VMEM((responses, length + 8, pair), F32),
             pltpu.VMEM((responses, length, channels), F32),
-            pltpu.VMEM((slices, rows, pair), F32),
-            pltpu.VMEM((slices, rows, pair), F32),
+            pltpu.VMEM((2, slices, rows, nstate), F32),
+            pltpu.VMEM((2, slices, rows, nstate), F32),
             pltpu.VMEM((peers, rows_fin, max(channels, nstate)), F32),
-            pltpu.VMEM((senders, 2 * depth + 2, nstate), F32),
+            pltpu.VMEM((2, senders, depth + 1, nstate), F32),
             pltpu.VMEM((slices, 2 * depth + 2, nstate), F32),
             pltpu.VMEM((groups, 2 * depth + 2, nstate), F32),
             pltpu.VMEM((responses, length, channels), F32),
@@ -588,10 +627,12 @@
             pltpu.VMEM((responses, heads, length, length), F32),
             pltpu.VMEM((responses, heads, length, length), F32),
             pltpu.VMEM((responses, length, length), F32),
-            pltpu.VMEM((responses, 2, length, channels), BF16),
-            dma((14,)),
+            pltpu.VMEM((responses, 2 * length, channels), BF16),
+            *(pltpu.VMEM((count // (4 * 128 * 4), 4, 128), F32) for count in (taken, sent)),
+            dma((10,)),
         ]
-        + [dma((2,))] * 7,
+        + [dma((1,))] * 6
+        + [dma((2,))] * 2,
         compiler_params=pltpu.CompilerParams(
             collective_id=0, has_side_effects=True
         ),

time: 19.6 us -> 19.4 us (0.990)
  the two profiles are of different devices: /device:TPU:7 before, /device:TPU:0 now
where the time goes in v3:
time: 19.4 us; the launch traced here: 19.1 us
  Pallas kernels  18.5 us (95%)
  between operations  0.65 us (3%)
    pallas_call x1, Pallas kernels, local(): pl.pallas_call(functools.partial(kernel, peers, slices, groups), out_shap...  17.8 us
    pallas_call x1, Pallas kernels, local(): pl.pallas_call(finish, out_shape=outs, in_specs=[vmem] * 6, out_specs=[an...  0.72 us

profile of v3, /device:TPU:0, one launch (start us, length us, event | category | flops | bytes accessed | tf_op | source)
XLA Modules:
  0.0 19.1 jit_solution(5488547182711332086)
XLA Ops:
  0.6 17.8 %shard_map.181 = (bf16[256,256]{1,0:T(8,128)(2,1)S(1)}, bf16[32,256]{1,0:T(8,128)(2,1)S(1)}, bf16[4,256]{1,0:T(4,128)(2,1)S(1)}, f32[4,256]{1,0:T(4,128)S(1)}, f32[4,256]{1,0:T(4,128)S(1)}, /*index=5*/f32[3,4]{1,0:T(4,128)S(1)}) custom-call(s32[2]{0:T(128)} %refs_0_.1, s32[2]{0:T(128)} %refs_1_.1, f32[4]{0:T(128)} %refs_2_.1, f32[4]{0:T(128)} %refs_3_.1, ...), custom_call_target="tpu_custom_call" | custom-call | tf_op jit(solution)/shard_map/pallas_call | solution.py:599
  18.4 0.7 %shard_map.182 = (bf16[256,256]{1,0:T(8,128)(2,1)}, bf16[32,256]{1,0:T(8,128)(2,1)}, bf16[4,256]{1,0:T(4,128)(2,1)}, f32[4,256]{1,0:T(4,128)}, f32[4,256]{1,0:T(4,128)}, /*index=5*/f32[3,4]{1,0:T(4,128)}) custom-call(bf16[256,256]{1,0:T(8,128)(2,1)S(1)} %get-tuple-element.12.refs_0_, bf16[32,256]{1,0:T(8,128)(2,1)S(1)} %get-tuple-element.13.refs_1_, ...), custom_call_target="tpu_custom_call" | custom-call | tf_op jit(solution)/shard_map/pallas_call | solution.py:641

commit v4 on v3

--- a/solution.py
+++ b/solution.py
@@ -8,7 +8,6 @@
 from jax.sharding import PartitionSpec as P
 
 DEV_GROUP = 8
-AHEAD = 1
 GROUP = 1
 MESH = pl.DeviceIdType.MESH
 F32 = jnp.float32
@@ -57,7 +56,7 @@
     (
     msg, state, gath, msg_out, state_out, pad_x, pad_bc, dpx, dpbc, dw_ref, raw, back,
     fin, all_taps, across_taps, sum_taps, x_act, x_slope, bc_slope, tap_rows, decays, products, score_grads, fed,
-    taken, sent,
+    taken, sent, starts, proj_rows, fence,
     sem_in, sem_out, sem_msg, sem_state, sem_gath, sem_back, sem_fin, sem_along, sem_across,
     ) = refs
     mine = lax.axis_index("exch")
@@ -169,15 +168,8 @@
     loads[sooner[-1]].wait()
     for k in range(peers - 1):
         fill_state(order[k], state_out.at[k])
-        if k < AHEAD:
-            remote(state_out.at[k], state.at[mine], sem_state, {"exch": order[k]})
+        remote(state_out.at[k], state.at[mine], sem_state, {"exch": order[k]})
     fill_state(mine, state.at[mine])
-
-    def send_states():
-        for k in range(AHEAD, peers - 1):
-            remote(state_out.at[k], state.at[mine], sem_state, {"exch": order[k]})
-
-    pl.when(lax.rem(me, 2) == 0)(send_states)
     gath[me] = group_columns(bc_ref, me)[...]
     for i in later:
         loads[i].wait()
@@ -341,6 +333,7 @@
         act, slope, windows = convolve(pad_bc, wbc, r, length)
         proj_b, proj_c = split(act[:, :half]), split(act[:, half:])
         projs.append((proj_b, proj_c))
+        proj_rows[r, 0:length], proj_rows[r, length:] = proj_c
         pre_grad = three(nn, grads[r], proj_c) * slope[:, :half]
         c_grad = three(nn, grads_t[r], proj_b)
         dpbc[r, 0:length, 0:half] = pre_grad
@@ -390,8 +383,6 @@
 
     send_taps(0, b_taps)
     send_bc(0)
-
-    pl.when(lax.rem(me, 2) == 1)(send_states)
     across_rows = jnp.zeros((lanes, length), F32)
     dt_first = jnp.zeros((lanes, length), F32)
     row_index = iota((lanes, 1), 0)
@@ -433,23 +424,25 @@
     for r in range(responses):
         sums = local_rows(r, *sums)
     settle(sem_state, 0, state.at[pl.ds(0, peers - 1)])
-    starts, lates = [], []
+    lates = []
     for r in range(responses):
         start = jnp.zeros(state.shape[1:], BF16)
         for z in range(peers):
             pick = weights[r // GROUP][z][:, : state.shape[2]].astype(BF16)
             start = start + state[z] * pick
-        starts.append(start)
+        starts[r] = start
         both = nn(fed[r], start)
         late = both[:length] + both[length:]
         lates.append(late)
         c_taps = c_taps + tap_sums(late, [tap_rows[r, k] for k in range(taps_n)])
     send_taps(1, c_taps)
+    pl.semaphore_signal(fence, inc=1)
+    pl.semaphore_wait(fence, 1)
     across_rows, dt_first, skip_sum, grad_wx = sums
     entry_grad = jnp.zeros((lanes, length), F32)
     for r in range(responses):
-        proj_c = projs[r][1]
-        carried = two(nt, proj_c, starts[r])
+        both = nt(proj_rows[r], starts[r])
+        carried = both[:length] + both[length:]
         prod = split(carried * cots[r])
         mark = indicator(r)
         entry_grad = entry_grad + (nt(mark, prod[0]) + nt(mark, prod[1]))
@@ -629,6 +622,9 @@
             pltpu.VMEM((responses, length, length), F32),
             pltpu.VMEM((responses, 2 * length, channels), BF16),
             *(pltpu.VMEM((count // (4 * 128 * 4), 4, 128), F32) for count in (taken, sent)),
+            pltpu.VMEM((responses, heads * width, nstate), BF16),
+            pltpu.VMEM((responses, 2 * length, nstate), BF16),
+            pltpu.SemaphoreType.REGULAR,
             dma((10,)),
         ]
         + [dma((1,))] * 6

time: 19.4 us -> 19.3 us (level)
  no operation moved by 1% of the time
where the time goes in v4:
time: 19.3 us; the launch traced here: 19 us
  Pallas kernels  18.4 us (95%)
  between operations  0.65 us (3%)
    pallas_call x1, Pallas kernels, local(): pl.pallas_call(functools.partial(kernel, peers, slices, groups), out_shap...  17.7 us
    pallas_call x1, Pallas kernels, local(): pl.pallas_call(finish, out_shape=outs, in_specs=[vmem] * 6, out_specs=[an...  0.72 us

profile of v4, /device:TPU:0, one launch (start us, length us, event | category | flops | bytes accessed | tf_op | source)
XLA Modules:
  0.0 19.0 jit_solution(16434451389129164689)
XLA Ops:
  0.6 17.7 %shard_map.181 = (bf16[256,256]{1,0:T(8,128)(2,1)S(1)}, bf16[32,256]{1,0:T(8,128)(2,1)S(1)}, bf16[4,256]{1,0:T(4,128)(2,1)S(1)}, f32[4,256]{1,0:T(4,128)S(1)}, f32[4,256]{1,0:T(4,128)S(1)}, /*index=5*/f32[3,4]{1,0:T(4,128)S(1)}) custom-call(s32[2]{0:T(128)} %refs_0_.1, s32[2]{0:T(128)} %refs_1_.1, f32[4]{0:T(128)} %refs_2_.1, f32[4]{0:T(128)} %refs_3_.1, ...), custom_call_target="tpu_custom_call" | custom-call | tf_op jit(solution)/shard_map/pallas_call | solution.py:592
  18.3 0.7 %shard_map.182 = (bf16[256,256]{1,0:T(8,128)(2,1)}, bf16[32,256]{1,0:T(8,128)(2,1)}, bf16[4,256]{1,0:T(4,128)(2,1)}, f32[4,256]{1,0:T(4,128)}, f32[4,256]{1,0:T(4,128)}, /*index=5*/f32[3,4]{1,0:T(4,128)}) custom-call(bf16[256,256]{1,0:T(8,128)(2,1)S(1)} %get-tuple-element.12.refs_0_, bf16[32,256]{1,0:T(8,128)(2,1)S(1)} %get-tuple-element.13.refs_1_, ...), custom_call_target="tpu_custom_call" | custom-call | tf_op jit(solution)/shard_map/pallas_call | solution.py:637

commit v5 on v4

--- a/solution.py
+++ b/solution.py
@@ -139,6 +139,9 @@
     for k in range(peers - 1):
         fill_msg(order[k], msg_out.at[k])
     fill_msg(mine, msg.at[mine])
+    loads[sooner[-1]].wait()
+    for k in range(peers - 1):
+        fill_state(order[k], state_out.at[k])
     pl.semaphore_wait(barrier, slices - 1 + peers - 1)
     def remote(src, dst, sem, where):
         shared = sem.shape[0] == 1
@@ -162,13 +165,11 @@
 
     for k in range(peers - 1):
         remote(msg_out.at[k], msg.at[mine], sem_msg, {"exch": order[k]})
+    for k in range(peers - 1):
+        remote(state_out.at[k], state.at[mine], sem_state, {"exch": order[k]})
     for o in range(1, slices):
         columns = group_columns(bc_ref, lax.rem(me + o, slices))
         remote(columns, gath.at[me], sem_gath, across(o))
-    loads[sooner[-1]].wait()
-    for k in range(peers - 1):
-        fill_state(order[k], state_out.at[k])
-        remote(state_out.at[k], state.at[mine], sem_state, {"exch": order[k]})
     fill_state(mine, state.at[mine])
     gath[me] = group_columns(bc_ref, me)[...]
     for i in later:

time: 19.3 us -> 19.3 us (level)
  no operation moved by 1% of the time
where the time goes in v5:
time: 19.3 us; the launch traced here: 19 us
  Pallas kernels  18.4 us (95%)
  between operations  0.65 us (3%)
    pallas_call x1, Pallas kernels, local(): pl.pallas_call(functools.partial(kernel, peers, slices, groups), out_shap...  17.7 us
    pallas_call x1, Pallas kernels, local(): pl.pallas_call(finish, out_shape=outs, in_specs=[vmem] * 6, out_specs=[an...  0.72 us

profile of v5, /device:TPU:0, one launch (start us, length us, event | category | flops | bytes accessed | tf_op | source)
XLA Modules:
  0.0 19.0 jit_solution(10145160917847052771)
XLA Ops:
  0.6 17.7 %shard_map.181 = (bf16[256,256]{1,0:T(8,128)(2,1)S(1)}, bf16[32,256]{1,0:T(8,128)(2,1)S(1)}, bf16[4,256]{1,0:T(4,128)(2,1)S(1)}, f32[4,256]{1,0:T(4,128)S(1)}, f32[4,256]{1,0:T(4,128)S(1)}, /*index=5*/f32[3,4]{1,0:T(4,128)S(1)}) custom-call(s32[2]{0:T(128)} %refs_0_.1, s32[2]{0:T(128)} %refs_1_.1, f32[4]{0:T(128)} %refs_2_.1, f32[4]{0:T(128)} %refs_3_.1, ...), custom_call_target="tpu_custom_call" | custom-call | tf_op jit(solution)/shard_map/pallas_call | solution.py:593
  18.3 0.7 %shard_map.182 = (bf16[256,256]{1,0:T(8,128)(2,1)}, bf16[32,256]{1,0:T(8,128)(2,1)}, bf16[4,256]{1,0:T(4,128)(2,1)}, f32[4,256]{1,0:T(4,128)}, f32[4,256]{1,0:T(4,128)}, /*index=5*/f32[3,4]{1,0:T(4,128)}) custom-call(bf16[256,256]{1,0:T(8,128)(2,1)S(1)} %get-tuple-element.12.refs_0_, bf16[32,256]{1,0:T(8,128)(2,1)S(1)} %get-tuple-element.13.refs_1_, ...), custom_call_target="tpu_custom_call" | custom-call | tf_op jit(solution)/shard_map/pallas_call | solution.py:638
